TPU v7x, 32 devices: a whole 2x2x4 slice. The times are simulated.
32 devices in a mesh: clip: 2 (over x), tm: 16 (over z, y, core).
Axes of the slice: x: 2, y: 2, z: 4, core: 2. Of those that a mesh axis runs over, the one named last changes fastest.
Arguments:
- tokens: bfloat16 [32768, 512], P(('clip', 'tm')), parts along dimension 0, may hold values from -6 to 6
- qkv_weight: bfloat16 [512, 1536], replicated, may hold values from -0.25 to 0.25
- out_weight: bfloat16 [512, 1024], replicated, may hold values from -0.25 to 0.25
- conv_weight: bfloat16 [3, 3, 256, 256], replicated, may hold values from -0.125 to 0.125
- norm_gain: float32 [256], replicated, may hold values from 0.25 to 1.75
- norm_bias: float32 [256], replicated, may hold values from -3 to 3
- group_map: int32 [32], P('clip'), parts along dimension 0, may hold values from 0 to 7, as said below
- token_order: int32 [2048], P('clip'), parts along dimension 0, may hold values from 0 to 1023, each once
- valid_frames: int32 [32], P('clip'), parts along dimension 0, may hold values from 1 to 16
Outputs:
- decoded: bfloat16 [32, 32, 128, 256], P('clip', 'tm'), parts along dimension 0
There are 2 independent parts, one for each index of `clip`. A program takes and returns all parts, laid end to end along the dimension named above; an argument that names none is the same for every part. Nothing has to cross between parts.
Inputs may be any that keep to these rules, and one draw needn't show every extreme that they name: `group_map`: never falls from one run to the next, and every group from 0 to 7 holds at least one run.
All inputs are finite; a program needn't handle non-finite values.
Results may differ from a plain program's by a relative error of at most 0.0055.
The roundings to bfloat16 on the way count: a program that leaves them out, or rounds other values in their place, can miss the bound.
Values may be sent and summed in bfloat16 or wider, within the bound.
A program may use at most 64 MiB of HBM per device.

v0:
```python
import functools

import jax
import jax.numpy as jnp
from jax import lax
from jax.experimental import pallas as pl
from jax.experimental.pallas import tpu as pltpu
from jax.sharding import PartitionSpec as P

HEADS = 16
NORM_GROUPS = 32
MESH = pl.DeviceIdType.MESH
F32 = jnp.float32
BF16 = jnp.bfloat16
CHUNK = 256
BLOCK = 256


def flat(cells):
    frames, rows, width = cells.shape
    if rows % 16 == 0:
        return cells.reshape(frames * rows, width)
    return cells.astype(F32).reshape(frames * rows, width).astype(BF16)


def mega(
    n,
    tokens_hbm,
    qkv_hbm,
    out_hbm,
    conv_hbm,
    gain_ref,
    group_ref,
    order_ref,
    valid_ref,
    conv_out,
    norm_ref,
    tokens_ref,
    qkv_ref,
    outw_ref,
    convw_ref,
    sent_tokens,
    tile_tokens,
    state_acc,
    sum_acc,
    sent_state,
    all_state,
    all_total,
    running,
    prefix,
    rows_ref,
    cells,
    halo,
    conv_acc,
    stat_acc,
    sent_stat,
    all_stat,
    out_buf,
    load_sem,
    tok_send,
    tok_recv,
    st_send,
    st_recv,
    pass_send,
    pass_recv,
    halo_send,
    halo_recv,
    stat_send,
    stat_recv,
    store_sem,
):
    me = lax.axis_index("tm")
    count, width = tokens_ref.shape
    row_tokens = count // n
    chunks = count // CHUNK
    frames_per = CHUNK // row_tokens
    head_dim = width // HEADS
    channels = gain_ref.shape[1]
    blocks = width // BLOCK
    heads_per = BLOCK // head_dim
    group_size = channels // NORM_GROUPS

    loads = [
        pltpu.make_async_copy(a, b, load_sem.at[i])
        for i, (a, b) in enumerate(
            [
                (tokens_hbm, tokens_ref),
                (qkv_hbm, qkv_ref),
                (out_hbm, outw_ref),
                (conv_hbm, convw_ref),
            ]
        )
    ]
    for load in loads:
        load.start()

    barrier = pltpu.get_barrier_semaphore()

    @pl.loop(1, n)
    def _(s):
        pl.semaphore_signal(
            barrier, inc=1, device_id={"tm": lax.rem(me + s, n)}, device_id_type=MESH
        )

    def exchange(s, src, dst, send_sem, recv_sem):
        return pltpu.make_async_remote_copy(
            src_ref=src,
            dst_ref=dst,
            send_sem=send_sem.at[s],
            recv_sem=recv_sem.at[s],
            device_id={"tm": lax.rem(me + s, n)},
            device_id_type=MESH,
        )

    def tok_copy(t):
        return pltpu.make_async_remote_copy(
            src_ref=sent_tokens.at[t],
            dst_ref=tile_tokens.at[me],
            send_sem=tok_send.at[t],
            recv_sem=tok_recv.at[me],
            device_id={"tm": t},
            device_id_type=MESH,
        )

    def tok_arrival(t):
        return pltpu.make_async_remote_copy(
            src_ref=sent_tokens.at[t],
            dst_ref=tile_tokens.at[t],
            send_sem=tok_send.at[t],
            recv_sem=tok_recv.at[t],
            device_id={"tm": t},
            device_id_type=MESH,
        )

    partner = me + 1 - 2 * lax.rem(me, 2)

    def state_copy(k):
        return pltpu.make_async_remote_copy(
            src_ref=sent_state,
            dst_ref=all_state.at[me],
            send_sem=st_send.at[k],
            recv_sem=st_recv.at[k],
            device_id={"tm": lax.rem(me + 2 * k, n)},
            device_id_type=MESH,
        )

    def state_pass(k):
        source = lax.rem(me + n - 2 * k, n)
        return pltpu.make_async_remote_copy(
            src_ref=all_state.at[source],
            dst_ref=all_state.at[source],
            send_sem=pass_send.at[k],
            recv_sem=pass_recv.at[k],
            device_id={"tm": partner},
            device_id_type=MESH,
        )

    own_pass = pltpu.make_async_remote_copy(
        src_ref=sent_state,
        dst_ref=all_state.at[me],
        send_sem=pass_send.at[0],
        recv_sem=pass_recv.at[0],
        device_id={"tm": partner},
        device_id_type=MESH,
    )

    def stat_copy(s):
        return exchange(s, sent_stat, all_stat.at[me], stat_send, stat_recv)

    half = chunks // 2
    near = lax.div(me, n // 2) * half
    far = half - near

    loads[0].wait()
    loads[1].wait()
    state_acc[...] = jnp.zeros_like(state_acc)
    sum_acc[...] = jnp.zeros_like(sum_acc)

    @pl.loop(0, chunks)
    def _(c):
        rows = pl.ds(pl.multiple_of(c * CHUNK, CHUNK), CHUNK)
        mixed = jnp.dot(
            tokens_ref[rows, :], qkv_ref[:, width : 3 * width], preferred_element_type=F32
        ).astype(BF16)
        keys = jnp.maximum(mixed[:, :width], jnp.zeros((), BF16))
        sum_acc[...] += keys.astype(F32).reshape(CHUNK // 8, 8, width).sum(axis=0)
        for b in range(blocks):
            lanes = slice(b * BLOCK, (b + 1) * BLOCK)
            state_acc[b] += lax.dot_general(
                keys[:, lanes],
                mixed[:, width + b * BLOCK : width + (b + 1) * BLOCK],
                (((0,), (0,)), ((), ())),
                preferred_element_type=F32,
            )

    head_row = lax.broadcasted_iota(jnp.int32, (BLOCK, BLOCK), 0) // head_dim
    head_col = lax.broadcasted_iota(jnp.int32, (BLOCK, BLOCK), 1) // head_dim
    same_head = head_row == head_col
    pieces = width // 128
    for b in range(blocks):
        own = jnp.where(same_head, state_acc[b], 0.0)
        own = own.reshape(heads_per, head_dim, BLOCK).sum(axis=0).astype(BF16)
        for i in range(BLOCK // 128):
            at = (b * (BLOCK // 128) + i) * head_dim
            sent_state[at : at + head_dim, :] = own[:, i * 128 : (i + 1) * 128]
    key_sum = jnp.sum(sum_acc[...], axis=0, keepdims=True)
    high = key_sum.astype(BF16).astype(F32)
    line = lax.broadcasted_iota(jnp.int32, (16, 128), 0)
    packed = jnp.zeros((16, 128), F32)
    for i in range(pieces):
        lanes = slice(i * 128, (i + 1) * 128)
        packed = jnp.where(line == i, high[:, lanes], packed)
        packed = jnp.where(line == pieces + i, (key_sum - high)[:, lanes], packed)
    sum_at = pieces * head_dim
    sent_state[sum_at : sum_at + 16, :] = packed.astype(BF16)

    pl.semaphore_wait(barrier, n - 1)

    @pl.loop(1, n // 2)
    def _(k):
        state_copy(k).start()

    own_pass.start()
    all_state[me] = sent_state[...]

    @pl.loop(0, chunks)
    def _(to):
        place = lax.broadcasted_iota(jnp.int32, (CHUNK, count), 0) + to * CHUNK
        pick = jnp.where(order_ref[...] == place, 1.0, 0.0).astype(BF16)
        moved = jnp.dot(pick, tokens_ref[...], preferred_element_type=F32)
        sent_tokens[pl.ds(to * frames_per, frames_per)] = moved.reshape(
            frames_per, row_tokens, width
        ).astype(BF16)

    for first in (near, far):

        @pl.loop(0, n // 2)
        def _(k):
            t = first * frames_per + lax.rem(me + k, n // 2)

            @pl.when(t != me)
            def _():
                tok_copy(t).start()

    tile_tokens[me] = sent_tokens[me]

    @pl.loop(1, n // 2)
    def _(k):
        state_copy(k).wait_recv()
        state_pass(k).start()

    @pl.loop(0, n // 2)
    def _(k):
        state_pass(k).wait_recv()

    running[...] = jnp.zeros_like(running)
    prefix[...] = jnp.zeros_like(prefix)

    @pl.loop(0, n)
    def _(f):
        new_group = group_ref[f] != group_ref[jnp.maximum(f - 1, 0)]
        before = jnp.where(new_group, running[...], prefix[...])
        prefix[...] = before
        own = all_state[f].astype(F32)
        running[...] += own
        all_total[f] = before + own

    valid_rows = valid_ref[me] * row_tokens
    loads[2].wait()

    def widen(even, odd):
        column = lax.rem(lax.broadcasted_iota(jnp.int32, even.shape, 0), row_tokens)
        odd_left = jnp.where(column == 0, 0.0, pltpu.roll(odd, 1, 0))
        even_right = jnp.where(column == row_tokens - 1, 0.0, pltpu.roll(even, CHUNK - 1, 0))
        return [x.astype(BF16) for x in (odd_left, even, odd, even_right)]

    def down_copy(c):
        rows = pl.ds(pl.multiple_of(c * CHUNK, CHUNK), CHUNK)
        return pltpu.make_async_remote_copy(
            src_ref=cells.at[1, rows, channels : 3 * channels],
            dst_ref=halo.at[0, rows, :],
            send_sem=halo_send.at[0, c],
            recv_sem=halo_recv.at[0, c],
            device_id={"tm": lax.rem(me + 1, n)},
            device_id_type=MESH,
        )

    def up_copy(c):
        rows = pl.ds(pl.multiple_of(c * CHUNK, CHUNK), CHUNK)
        return pltpu.make_async_remote_copy(
            src_ref=cells.at[0, rows, channels : 3 * channels],
            dst_ref=halo.at[1, rows, :],
            send_sem=halo_send.at[1, c],
            recv_sem=halo_recv.at[1, c],
            device_id={"tm": lax.rem(me + n - 1, n)},
            device_id_type=MESH,
        )

    head_ones = same_head.astype(F32).astype(BF16)
    reach = 3 * channels
    loads[3].wait()

    def advance(c):
        rows = pl.ds(pl.multiple_of(c * CHUNK, CHUNK), CHUNK)

        @pl.loop(0, frames_per)
        def _(k):
            t = c * frames_per + k

            @pl.when(t != me)
            def _():
                tok_arrival(t).wait_recv()

        mixed = jnp.dot(
            flat(tile_tokens[pl.ds(c * frames_per, frames_per)]),
            qkv_ref[:, 0:width],
            preferred_element_type=F32,
        ).astype(BF16)
        rows_ref[...] = jnp.maximum(mixed, jnp.zeros((), BF16)).astype(F32)

        def attend(k, carry):
            f = c * frames_per + k
            total = all_total[f]
            key_total = jnp.concatenate(
                [
                    total[sum_at + i : sum_at + i + 1, :]
                    + total[sum_at + pieces + i : sum_at + pieces + i + 1, :]
                    for i in range(pieces)
                ],
                axis=1,
            )
            here = pl.ds(pl.multiple_of(k * row_tokens, 8), row_tokens)
            query = rows_ref[here, :]
            scaled = (query * key_total).astype(BF16)
            query = query.astype(BF16)
            for b in range(blocks):
                lanes = slice(b * BLOCK, (b + 1) * BLOCK)
                first = b * (BLOCK // 128)
                state = jnp.concatenate(
                    [
                        total[i * head_dim : (i + 1) * head_dim, :]
                        for i in range(first, first + BLOCK // 128)
                    ],
                    axis=1,
                )
                high = state.astype(BF16).astype(F32)
                numer = jnp.zeros((row_tokens, BLOCK), F32)
                for part in (high, state - high):
                    spread = jnp.concatenate([part] * heads_per, axis=0)
                    spread = jnp.where(same_head, spread, 0.0).astype(BF16)
                    numer += jnp.dot(query[:, lanes], spread, preferred_element_type=F32)
                denom = jnp.dot(scaled[:, lanes], head_ones, preferred_element_type=F32) + 1.0
                rows_ref[here, lanes] = numer / denom
            return carry

        lax.fori_loop(0, frames_per, attend, 0, unroll=frames_per <= 4)
        mapped = jnp.dot(rows_ref[...].astype(BF16), outw_ref[...], preferred_element_type=F32)
        row = lax.broadcasted_iota(jnp.int32, mapped.shape, 0) + c * CHUNK
        mapped = jnp.where(row < valid_rows, mapped, 0.0)
        for a in range(2):
            even = mapped[:, 2 * a * channels : (2 * a + 1) * channels]
            odd = mapped[:, (2 * a + 1) * channels : (2 * a + 2) * channels]
            for i, part in enumerate(widen(even, odd)):
                cells[a, rows, i * channels : (i + 1) * channels] = part

        @pl.when(me < n - 1)
        def _():
            down_copy(c).start()

        @pl.when(me > 0)
        def _():
            up_copy(c).start()

        for r in range(2):
            for b in range(2):
                lanes = slice(b * channels, b * channels + reach)
                conv_acc[r, rows, b * channels : (b + 1) * channels] = jnp.dot(
                    cells[0, rows, lanes], convw_ref[1 - r], preferred_element_type=F32
                ) + jnp.dot(cells[1, rows, lanes], convw_ref[2 - r], preferred_element_type=F32)

    @pl.loop(0, half)
    def _(k):
        advance(near + k)

    @pl.loop(0, half)
    def _(k):
        advance(far + k)

    @pl.when(me == 0)
    def _():
        halo[0] = jnp.zeros(halo.shape[1:], BF16)

    @pl.when(me == n - 1)
    def _():
        halo[1] = jnp.zeros(halo.shape[1:], BF16)

    def store(f, r, h):
        pixels = pl.ds(pl.multiple_of(f * 2 * row_tokens, 8), 2 * row_tokens)
        return pltpu.make_async_copy(
            out_buf.at[r, h, pixels, :],
            conv_out.at[f, r, :, h * 128 : (h + 1) * 128],
            store_sem.at[f, r, h],
        )

    sides = [(r, h) for r in range(2) for h in range(channels // 128)]

    stat_acc[...] = jnp.zeros_like(stat_acc)

    @pl.loop(0, chunks)
    def _(c):
        rows = pl.ds(pl.multiple_of(c * CHUNK, CHUNK), CHUNK)

        @pl.when(me > 0)
        def _():
            down_copy(c).wait_recv()

        @pl.when(me < n - 1)
        def _():
            up_copy(c).wait_recv()

        row = lax.broadcasted_iota(jnp.int32, (CHUNK, channels), 0) + c * CHUNK
        for r in range(2):
            edge = halo[r, rows, :].astype(F32)
            parts = widen(edge[:, :channels], edge[:, channels:])
            for b in range(2):
                taps = jnp.concatenate(parts[b : b + 3], axis=1)
                lanes = slice(b * channels, (b + 1) * channels)
                result = conv_acc[r, rows, lanes] + jnp.dot(
                    taps, convw_ref[2 * r], preferred_element_type=F32
                )
                result = jnp.where(row < valid_rows, result, 0.0)
                for h in range(0, channels, 128):
                    out_buf[r, h // 128, pl.ds(c * 2 * CHUNK + b, CHUNK, 2), :] = result[
                        :, h : h + 128
                    ]
                stat_acc[0] += result.reshape(CHUNK // 8, 8, channels).sum(axis=0)

    @pl.loop(0, n)
    def _(f):
        for r, h in sides:
            store(f, r, h).start()

    unit = (4 * row_tokens * group_size)
    group_row = lax.broadcasted_iota(jnp.int32, (channels, channels), 0) // group_size
    group_col = lax.broadcasted_iota(jnp.int32, (channels, channels), 1) // group_size
    group_ones = (group_row == group_col).astype(F32)

    def group_total(part):
        sums = jnp.sum(part, axis=0, keepdims=True)
        return jnp.dot(
            jnp.broadcast_to(sums, (8, channels)),
            group_ones,
            precision=lax.Precision.HIGHEST,
            preferred_element_type=F32,
        )

    tile_sum = group_total(stat_acc[0])
    tile_mean = tile_sum[0:1, :] / (valid_ref[me] * unit).astype(F32)

    @pl.loop(0, 2 * chunks)
    def _(c):
        pixels = pl.ds(pl.multiple_of(c * CHUNK, CHUNK), CHUNK)
        row = lax.broadcasted_iota(jnp.int32, (CHUNK, 128), 0) + c * CHUNK
        for r, h in sides:
            lanes = slice(h * 128, (h + 1) * 128)
            off = jnp.where(row < 2 * valid_rows, out_buf[r, h, pixels, :] - tile_mean[:, lanes], 0.0)
            stat_acc[1, :, lanes] += (off * off).reshape(CHUNK // 8, 8, 128).sum(axis=0)

    tile_square = group_total(stat_acc[1])
    line = lax.broadcasted_iota(jnp.int32, (8, channels), 0)
    sent_stat[...] = jnp.where(line == 0, tile_sum, tile_square)

    @pl.loop(1, n)
    def _(s):
        stat_copy(s).start()

    all_stat[me] = sent_stat[...]

    @pl.loop(1, n)
    def _(s):
        stat_copy(s).wait_recv()

    def add_sum(t, carry):
        total, units = carry
        return total + all_stat[t, 0:1, :], units + valid_ref[t]

    total, units = lax.fori_loop(
        0, n, add_sum, (jnp.zeros((1, channels), F32), jnp.zeros((), jnp.int32))
    )
    total_count = units.astype(F32) * unit
    mean = total / total_count

    def add_square(t, square):
        size = (valid_ref[t] * unit).astype(F32)
        off = all_stat[t, 0:1, :] / size - mean
        return square + all_stat[t, 1:2, :] + size * (off * off)

    square = lax.fori_loop(0, n, add_square, jnp.zeros((1, channels), F32))
    scale = gain_ref[...] * lax.rsqrt(square / total_count + 1e-05)
    norm_ref[...] = jnp.where(
        line == 0, mean, jnp.where(line == 1, scale, valid_ref[me].astype(F32))
    )

    @pl.loop(0, n)
    def _(f):
        for r, h in sides:
            store(f, r, h).wait()

    @pl.loop(0, chunks)
    def _(c):
        @pl.when(me < n - 1)
        def _():
            down_copy(c).wait_send()

        @pl.when(me > 0)
        def _():
            up_copy(c).wait_send()

    @pl.loop(1, n)
    def _(s):
        tok_copy(lax.rem(me + s, n)).wait_send()
        stat_copy(s).wait_send()

    own_pass.wait_send()

    @pl.loop(1, n // 2)
    def _(k):
        state_copy(k).wait_send()
        state_pass(k).wait_send()


def local(
    tokens,
    qkv_weight,
    out_weight,
    conv_weight,
    norm_gain,
    norm_bias,
    group_map,
    token_order,
    valid_frames,
):
    n = lax.axis_size("tm")
    count, width = tokens.shape
    channels = conv_weight.shape[3]
    row_tokens = count // n
    chunks = count // CHUNK
    state_shape = (width // 128 * (width // HEADS) + 16, 128)
    anywhere = pl.BlockSpec(memory_space=pl.ANY)
    vmem = pl.BlockSpec(memory_space=pltpu.VMEM)
    smem = pl.BlockSpec(memory_space=pltpu.SMEM)
    dma = pltpu.SemaphoreType.DMA
    conv, norm = pl.pallas_call(
        functools.partial(mega, n),
        out_shape=(
            jax.ShapeDtypeStruct((n, 2, 2 * row_tokens, channels), F32),
            jax.ShapeDtypeStruct((8, channels), F32),
        ),
        in_specs=[anywhere] * 4 + [vmem, smem, vmem, smem],
        out_specs=(anywhere, vmem),
        scratch_shapes=[
            pltpu.VMEM((count, width), BF16),
            pltpu.VMEM((width, 3 * width), BF16),
            pltpu.VMEM((width, 4 * channels), BF16),
            pltpu.VMEM((3, 3 * channels, channels), BF16),
            pltpu.VMEM((n, row_tokens, width), BF16),
            pltpu.VMEM((n, row_tokens, width), BF16),
            pltpu.VMEM((width // BLOCK, BLOCK, BLOCK), F32),
            pltpu.VMEM((8, width), F32),
            pltpu.VMEM(state_shape, BF16),
            pltpu.VMEM((n,) + state_shape, BF16),
            pltpu.VMEM((n,) + state_shape, F32),
            pltpu.VMEM(state_shape, F32),
            pltpu.VMEM(state_shape, F32),
            pltpu.VMEM((CHUNK, width), F32),
            pltpu.VMEM((2, count, 4 * channels), BF16),
            pltpu.VMEM((2, count, 2 * channels), BF16),
            pltpu.VMEM((2, count, 2 * channels), F32),
            pltpu.VMEM((2, 8, channels), F32),
            pltpu.VMEM((8, channels), F32),
            pltpu.VMEM((n, 8, channels), F32),
            pltpu.VMEM((2, channels // 128, 2 * count, 128), F32),
            dma((4,)),
            dma((n,)),
            dma((n,)),
            dma((n // 2,)),
            dma((n // 2,)),
            dma((n // 2,)),
            dma((n // 2,)),
            dma((2, chunks)),
            dma((2, chunks)),
            dma((n,)),
            dma((n,)),
            dma((n, 2, channels // 128)),
        ],
        compiler_params=pltpu.CompilerParams(
            collective_id=0, has_side_effects=True, vmem_limit_bytes=60 * 1024 * 1024
        ),
    )(
        tokens,
        qkv_weight,
        out_weight,
        conv_weight.reshape(3, 3 * channels, channels),
        norm_gain[None],
        group_map,
        token_order[None],
        valid_frames,
    )
    frame = lax.broadcasted_iota(jnp.int32, conv.shape, 0).astype(F32)
    normed = (conv - norm[0]) * norm[1] + norm_bias
    return jnp.where(frame < norm[2], jax.nn.silu(normed), 0.0).astype(BF16)


def solution(mesh):
    in_specs = (P(("clip", "tm"), None), P(), P(), P(), P(), P(), P("clip"), P("clip"), P("clip"))
    out_specs = P("clip", "tm", None, None)
    return jax.shard_map(local, mesh=mesh, in_specs=in_specs, out_specs=out_specs, check_vma=False)
```

profile of v0, /device:TPU:0, one launch (start us, length us, event | category | flops | bytes accessed | tf_op | source)
XLA Modules:
  0.0 70.6 jit_solution(5215081791993592138)
XLA Ops:
  0.0 0.0 copy-start
  0.0 64.8 %shard_map.91 = (f32[16,2,128,256]{3,2,1,0:T(8,128)}, f32[8,256]{1,0:T(8,128)}) custom-call(bf16[1024,512]{1,0:T(8,128)(2,1)} %tokens_hbm.1, bf16[512,1536]{1,0:T(8,128)(2,1)} %qkv_hbm.1, bf16[512,1024]{1,0:T(8,128)(2,1)} %out_hbm.1, bf16[3,768,256]{2,1,0:T(8,128)(2,1)} %bitcast.6, f32[1,256]{1,0:T(1,128)} %bitcast.11, s32[16]{0:T(128)} %group_ref.1, ...), custom_call_target="tpu_custom_call" | custom-call | tf_op jit(solution)/shard_map/pallas_call | solution.py:553
  64.8 0.8 %fusion = (f32[1,256]{1,0:T(1,128)S(1)}, f32[1,256]{1,0:T(1,128)S(1)}, f32[1,256]{1,0:T(1,128)S(1)}) fusion(f32[8,256]{1,0:T(8,128)} %get-tuple-element.7), kind=kLoop, calls=%fused_computation.2 | loop fusion | bytes 6144 | tf_op jit(solution)/shard_map/slice | solution.py:611
  65.7 0.0 copy-done
  65.7 4.9 %select_convert_fusion = bf16[16,2,128,256]{3,2,1,0:T(8,128)(2,1)} fusion(f32[16,2,128,256]{3,2,1,0:T(8,128)} %get-tuple-element.8, f32[256]{0:T(256)S(1)} %copy-done, f32[256]{0:T(256)S(1)} %bitcast.9, f32[256]{0:T(256)S(1)} %bitcast.10, f32[256]{0:T(256)S(1)} %bitcast.8, f32[16]{0:T(128)S(1)} %iota_convert_fusion), kind=kLoop, calls=%fused_computation | loop fusion | flops 10485760 | bytes 6295616 | tf_op jit(solution)/shard_map/convert_element_type | solution.py:611
  (1 shorter events, 0.0 us)
Async XLA Ops:
  0.0 65.7 %copy-start = (f32[256]{0:T(256)S(1)}, f32[256]{0:T(256)}, u32[]{:S(2)}) copy-start(f32[256]{0:T(256)} %param.14) | copy-start | bytes 3076
where the time goes:
time: 70.8 us; the launch traced here: 70.6 us
  Pallas kernels  64.8 us (92%)
  other arithmetic  4.9 us (7%)
  local copies, waits for them, and re-layouts  0.82 us (1%)
    pallas_call x1, Pallas kernels, local(): pl.pallas_call(functools.partial(mega, n), out_shape=(jax.ShapeDtypeStruc...  64.8 us
    convert_element_type x1, other arithmetic, local(): return jnp.where(frame < norm[2], jax.nn.silu(normed), 0.0).astype(BF16)  4.9 us

commit v1 on v0

--- a/solution.py
+++ b/solution.py
@@ -14,6 +14,7 @@
 BF16 = jnp.bfloat16
 CHUNK = 256
 BLOCK = 256
+VMEM = 66650112
 
 
 def flat(cells):
@@ -30,11 +31,11 @@
     out_hbm,
     conv_hbm,
     gain_ref,
+    bias_ref,
     group_ref,
     order_ref,
     valid_ref,
-    conv_out,
-    norm_ref,
+    decoded_ref,
     tokens_ref,
     qkv_ref,
     outw_ref,
@@ -59,15 +60,16 @@
     load_sem,
     tok_send,
     tok_recv,
-    st_send,
-    st_recv,
-    pass_send,
-    pass_recv,
+    core_send,
+    core_recv,
+    col_send,
+    col_recv,
+    row_send,
+    row_recv,
     halo_send,
     halo_recv,
     stat_send,
     stat_recv,
-    store_sem,
 ):
     me = lax.axis_index("tm")
     count, width = tokens_ref.shape
@@ -132,43 +134,44 @@
             device_id_type=MESH,
         )
 
-    partner = me + 1 - 2 * lax.rem(me, 2)
-
-    def state_copy(k):
+    levels = n // 4
+    core_peer = me + 1 - 2 * lax.rem(me, 2)
+    row_peer = me + 2 - 4 * lax.rem(lax.div(me, 2), 2)
+
+    def column_copy(k):
         return pltpu.make_async_remote_copy(
             src_ref=sent_state,
             dst_ref=all_state.at[me],
-            send_sem=st_send.at[k],
-            recv_sem=st_recv.at[k],
-            device_id={"tm": lax.rem(me + 2 * k, n)},
+            send_sem=col_send.at[k],
+            recv_sem=col_recv.at[k],
+            device_id={"tm": lax.rem(me + 4 * k, n)},
             device_id_type=MESH,
         )
 
-    def state_pass(k):
-        source = lax.rem(me + n - 2 * k, n)
+    def pass_on(source, peer, send_sem, recv_sem):
         return pltpu.make_async_remote_copy(
             src_ref=all_state.at[source],
             dst_ref=all_state.at[source],
-            send_sem=pass_send.at[k],
-            recv_sem=pass_recv.at[k],
-            device_id={"tm": partner},
+            send_sem=send_sem,
+            recv_sem=recv_sem,
+            device_id={"tm": peer},
             device_id_type=MESH,
         )
 
-    own_pass = pltpu.make_async_remote_copy(
-        src_ref=sent_state,
-        dst_ref=all_state.at[me],
-        send_sem=pass_send.at[0],
-        recv_sem=pass_recv.at[0],
-        device_id={"tm": partner},
-        device_id_type=MESH,
-    )
+    def row_pass(k):
+        source = lax.rem(me + n - 4 * k, n)
+        return pass_on(source, row_peer, row_send.at[k], row_recv.at[k])
+
+    def core_pass(k, d):
+        source = lax.rem(me + d * (row_peer - me) + n - 4 * k, n)
+        return pass_on(source, core_peer, core_send.at[d, k], core_recv.at[d, k])
 
     def stat_copy(s):
         return exchange(s, sent_stat, all_stat.at[me], stat_send, stat_recv)
 
     half = chunks // 2
-    near = lax.div(me, n // 2) * half
+    side = lax.div(me, n // 2)
+    near = side * half
     far = half - near
 
     loads[0].wait()
@@ -197,6 +200,7 @@
     head_col = lax.broadcasted_iota(jnp.int32, (BLOCK, BLOCK), 1) // head_dim
     same_head = head_row == head_col
     pieces = width // 128
+    sum_at = pieces * head_dim
     for b in range(blocks):
         own = jnp.where(same_head, state_acc[b], 0.0)
         own = own.reshape(heads_per, head_dim, BLOCK).sum(axis=0).astype(BF16)
@@ -211,20 +215,19 @@
         lanes = slice(i * 128, (i + 1) * 128)
         packed = jnp.where(line == i, high[:, lanes], packed)
         packed = jnp.where(line == pieces + i, (key_sum - high)[:, lanes], packed)
-    sum_at = pieces * head_dim
     sent_state[sum_at : sum_at + 16, :] = packed.astype(BF16)
 
+    all_state[me] = sent_state[...]
     pl.semaphore_wait(barrier, n - 1)
 
-    @pl.loop(1, n // 2)
-    def _(k):
-        state_copy(k).start()
-
-    own_pass.start()
-    all_state[me] = sent_state[...]
-
-    @pl.loop(0, chunks)
-    def _(to):
+    @pl.loop(1, levels)
+    def _(k):
+        column_copy(k).start()
+
+    row_pass(0).start()
+    core_pass(0, 0).start()
+
+    def permute(to):
         place = lax.broadcasted_iota(jnp.int32, (CHUNK, count), 0) + to * CHUNK
         pick = jnp.where(order_ref[...] == place, 1.0, 0.0).astype(BF16)
         moved = jnp.dot(pick, tokens_ref[...], preferred_element_type=F32)
@@ -232,26 +235,68 @@
             frames_per, row_tokens, width
         ).astype(BF16)
 
-    for first in (near, far):
-
-        @pl.loop(0, n // 2)
+    def near_tile(k):
+        return near * frames_per + lax.rem(me + k, n // 2)
+
+    def far_tile(k):
+        return far * frames_per + lax.rem(me + k, n // 2)
+
+    @pl.loop(0, half)
+    def _(k):
+        permute(near + k)
+
+    @pl.loop(1, n // 2)
+    def _(k):
+        tok_copy(near_tile(k)).start()
+
+    tile_tokens[me] = sent_tokens[me]
+
+    @pl.loop(0, half)
+    def _(k):
+        permute(far + k)
+
+    @pl.loop(0, n // 2)
+    def _(k):
+        tok_copy(far_tile(k)).start()
+
+    @pl.loop(1, levels)
+    def _(k):
+        column_copy(k).wait_recv()
+        row_pass(k).start()
+        core_pass(k, 0).start()
+
+    @pl.loop(0, levels)
+    def _(k):
+        row_pass(k).wait_recv()
+        core_pass(k, 1).start()
+
+    def chunk_rows(c):
+        return pl.ds(pl.multiple_of(c * CHUNK, CHUNK), CHUNK)
+
+    def queries(c):
+        @pl.loop(0, frames_per)
         def _(k):
-            t = first * frames_per + lax.rem(me + k, n // 2)
+            t = c * frames_per + k
 
             @pl.when(t != me)
             def _():
-                tok_copy(t).start()
-
-    tile_tokens[me] = sent_tokens[me]
-
-    @pl.loop(1, n // 2)
-    def _(k):
-        state_copy(k).wait_recv()
-        state_pass(k).start()
-
-    @pl.loop(0, n // 2)
-    def _(k):
-        state_pass(k).wait_recv()
+                tok_arrival(t).wait_recv()
+
+        mixed = jnp.dot(
+            flat(tile_tokens[pl.ds(c * frames_per, frames_per)]),
+            qkv_ref[:, 0:width],
+            preferred_element_type=F32,
+        ).astype(BF16)
+        rows_ref[chunk_rows(c), :] = jnp.maximum(mixed, jnp.zeros((), BF16)).astype(F32)
+
+    @pl.loop(0, half)
+    def _(k):
+        queries(near + k)
+
+    @pl.loop(0, levels)
+    def _(k):
+        core_pass(k, 0).wait_recv()
+        core_pass(k, 1).wait_recv()
 
     running[...] = jnp.zeros_like(running)
     prefix[...] = jnp.zeros_like(prefix)
@@ -300,23 +345,8 @@
     reach = 3 * channels
     loads[3].wait()
 
-    def advance(c):
-        rows = pl.ds(pl.multiple_of(c * CHUNK, CHUNK), CHUNK)
-
-        @pl.loop(0, frames_per)
-        def _(k):
-            t = c * frames_per + k
-
-            @pl.when(t != me)
-            def _():
-                tok_arrival(t).wait_recv()
-
-        mixed = jnp.dot(
-            flat(tile_tokens[pl.ds(c * frames_per, frames_per)]),
-            qkv_ref[:, 0:width],
-            preferred_element_type=F32,
-        ).astype(BF16)
-        rows_ref[...] = jnp.maximum(mixed, jnp.zeros((), BF16)).astype(F32)
+    def project(c):
+        rows = chunk_rows(c)
 
         def attend(k, carry):
             f = c * frames_per + k
@@ -329,7 +359,7 @@
                 ],
                 axis=1,
             )
-            here = pl.ds(pl.multiple_of(k * row_tokens, 8), row_tokens)
+            here = pl.ds(pl.multiple_of(f * row_tokens, 8), row_tokens)
             query = rows_ref[here, :]
             scaled = (query * key_total).astype(BF16)
             query = query.astype(BF16)
@@ -354,7 +384,7 @@
             return carry
 
         lax.fori_loop(0, frames_per, attend, 0, unroll=frames_per <= 4)
-        mapped = jnp.dot(rows_ref[...].astype(BF16), outw_ref[...], preferred_element_type=F32)
+        mapped = jnp.dot(rows_ref[rows, :].astype(BF16), outw_ref[...], preferred_element_type=F32)
         row = lax.broadcasted_iota(jnp.int32, mapped.shape, 0) + c * CHUNK
         mapped = jnp.where(row < valid_rows, mapped, 0.0)
         for a in range(2):
@@ -371,6 +401,8 @@
         def _():
             up_copy(c).start()
 
+    def convolve(c):
+        rows = chunk_rows(c)
         for r in range(2):
             for b in range(2):
                 lanes = slice(b * channels, b * channels + reach)
@@ -378,13 +410,55 @@
                     cells[0, rows, lanes], convw_ref[1 - r], preferred_element_type=F32
                 ) + jnp.dot(cells[1, rows, lanes], convw_ref[2 - r], preferred_element_type=F32)
 
-    @pl.loop(0, half)
-    def _(k):
-        advance(near + k)
-
-    @pl.loop(0, half)
-    def _(k):
-        advance(far + k)
+    def finish(c, r):
+        rows = chunk_rows(c)
+
+        if r == 0:
+
+            @pl.when(me > 0)
+            def _():
+                down_copy(c).wait_recv()
+
+        else:
+
+            @pl.when(me < n - 1)
+            def _():
+                up_copy(c).wait_recv()
+
+        row = lax.broadcasted_iota(jnp.int32, (CHUNK, channels), 0) + c * CHUNK
+        edge = halo[r, rows, :].astype(F32)
+        parts = widen(edge[:, :channels], edge[:, channels:])
+        results = []
+        for b in range(2):
+            taps = jnp.concatenate(parts[b : b + 3], axis=1)
+            lanes = slice(b * channels, (b + 1) * channels)
+            result = conv_acc[r, rows, lanes] + jnp.dot(
+                taps, convw_ref[2 * r], preferred_element_type=F32
+            )
+            result = jnp.where(row < valid_rows, result, 0.0)
+            results.append(result)
+            for h in range(0, channels, 128):
+                out_buf[r, h // 128, pl.ds(c * 2 * CHUNK + b, CHUNK, 2), :] = result[
+                    :, h : h + 128
+                ]
+        eights = [x.reshape(CHUNK // 8, 8, channels).sum(axis=0) for x in results]
+        total = jnp.sum(eights[0] + eights[1], axis=0, keepdims=True)
+        size = jnp.clip(valid_rows - c * CHUNK, 0, CHUNK) * 2
+        centre = total / jnp.maximum(size, 1).astype(F32)
+        square = jnp.zeros((8, channels), F32)
+        for x in results:
+            off = jnp.where(row < valid_rows, x - centre, 0.0)
+            square += (off * off).reshape(CHUNK // 8, 8, channels).sum(axis=0)
+        square = jnp.sum(square, axis=0, keepdims=True)
+        line = lax.broadcasted_iota(jnp.int32, (8, channels), 0)
+        stat_acc[2 * c + r] = jnp.where(
+            line == 0, total, jnp.where(line == 1, square, size.astype(F32))
+        )
+
+    inside = [me != n // 2, me != n // 2 - 1]
+
+    def far_chunk(k):
+        return far + k + side * (half - 1 - 2 * k)
 
     @pl.when(me == 0)
     def _():
@@ -394,81 +468,74 @@
     def _():
         halo[1] = jnp.zeros(halo.shape[1:], BF16)
 
-    def store(f, r, h):
-        pixels = pl.ds(pl.multiple_of(f * 2 * row_tokens, 8), 2 * row_tokens)
-        return pltpu.make_async_copy(
-            out_buf.at[r, h, pixels, :],
-            conv_out.at[f, r, :, h * 128 : (h + 1) * 128],
-            store_sem.at[f, r, h],
-        )
-
-    sides = [(r, h) for r in range(2) for h in range(channels // 128)]
-
-    stat_acc[...] = jnp.zeros_like(stat_acc)
-
-    @pl.loop(0, chunks)
-    def _(c):
-        rows = pl.ds(pl.multiple_of(c * CHUNK, CHUNK), CHUNK)
-
-        @pl.when(me > 0)
+    @pl.loop(0, half)
+    def _(k):
+        project(near + k)
+
+    @pl.loop(0, half)
+    def _(k):
+        convolve(near + k)
+
+    @pl.loop(0, half)
+    def _(k):
+        c = far_chunk(k)
+        queries(c)
+        project(c)
+        convolve(c)
+
+        for r in range(2):
+
+            @pl.when(inside[r])
+            def _():
+                finish(jnp.where(k == 0, near, far_chunk(k - 1)), r)
+
+                @pl.when(k == 0)
+                def _():
+                    finish(near + 1, r)
+
+    for r in range(2):
+
+        @pl.when(inside[r])
         def _():
-            down_copy(c).wait_recv()
-
-        @pl.when(me < n - 1)
+            finish(far_chunk(half - 1), r)
+
+        @pl.when(jnp.logical_not(inside[r]))
         def _():
-            up_copy(c).wait_recv()
-
-        row = lax.broadcasted_iota(jnp.int32, (CHUNK, channels), 0) + c * CHUNK
-        for r in range(2):
-            edge = halo[r, rows, :].astype(F32)
-            parts = widen(edge[:, :channels], edge[:, channels:])
-            for b in range(2):
-                taps = jnp.concatenate(parts[b : b + 3], axis=1)
-                lanes = slice(b * channels, (b + 1) * channels)
-                result = conv_acc[r, rows, lanes] + jnp.dot(
-                    taps, convw_ref[2 * r], preferred_element_type=F32
-                )
-                result = jnp.where(row < valid_rows, result, 0.0)
-                for h in range(0, channels, 128):
-                    out_buf[r, h // 128, pl.ds(c * 2 * CHUNK + b, CHUNK, 2), :] = result[
-                        :, h : h + 128
-                    ]
-                stat_acc[0] += result.reshape(CHUNK // 8, 8, channels).sum(axis=0)
-
-    @pl.loop(0, n)
-    def _(f):
-        for r, h in sides:
-            store(f, r, h).start()
-
-    unit = (4 * row_tokens * group_size)
+            @pl.loop(0, half)
+            def _(k):
+                finish(far + k, r)
+
+            @pl.loop(0, half)
+            def _(k):
+                finish(near + k + (1 - side) * (half - 1 - 2 * k), r)
+
     group_row = lax.broadcasted_iota(jnp.int32, (channels, channels), 0) // group_size
     group_col = lax.broadcasted_iota(jnp.int32, (channels, channels), 1) // group_size
-    group_ones = (group_row == group_col).astype(F32)
-
-    def group_total(part):
-        sums = jnp.sum(part, axis=0, keepdims=True)
-        return jnp.dot(
-            jnp.broadcast_to(sums, (8, channels)),
-            group_ones,
-            precision=lax.Precision.HIGHEST,
-            preferred_element_type=F32,
-        )
-
-    tile_sum = group_total(stat_acc[0])
-    tile_mean = tile_sum[0:1, :] / (valid_ref[me] * unit).astype(F32)
-
-    @pl.loop(0, 2 * chunks)
-    def _(c):
-        pixels = pl.ds(pl.multiple_of(c * CHUNK, CHUNK), CHUNK)
-        row = lax.broadcasted_iota(jnp.int32, (CHUNK, 128), 0) + c * CHUNK
-        for r, h in sides:
-            lanes = slice(h * 128, (h + 1) * 128)
-            off = jnp.where(row < 2 * valid_rows, out_buf[r, h, pixels, :] - tile_mean[:, lanes], 0.0)
-            stat_acc[1, :, lanes] += (off * off).reshape(CHUNK // 8, 8, 128).sum(axis=0)
-
-    tile_square = group_total(stat_acc[1])
+    group_ones = jnp.where(group_row == group_col, 1.0, 0.0).astype(BF16)
+
+    def group_total(sums):
+        parts = []
+        for _ in range(3):
+            part = sums.astype(BF16)
+            parts.append(part)
+            sums = sums - part.astype(F32)
+        line = lax.broadcasted_iota(jnp.int32, (16, channels), 0)
+        stacked = jnp.zeros((16, channels), F32)
+        for i, part in enumerate(parts):
+            stacked = jnp.where(line == i, part.astype(F32), stacked)
+        found = jnp.dot(stacked.astype(BF16), group_ones, preferred_element_type=F32)
+        return found[0:1] + found[1:2] + found[2:3]
+
+    def combine(field):
+        total, square, size = [field[:, i, :] for i in range(3)]
+        whole = jnp.sum(size, axis=0, keepdims=True)
+        mean = jnp.sum(total, axis=0, keepdims=True) / whole
+        off = total / jnp.maximum(size, 1.0) - mean
+        return mean, jnp.sum(square + size * (off * off), axis=0, keepdims=True), whole
+
+    mean, square, whole = combine(stat_acc)
     line = lax.broadcasted_iota(jnp.int32, (8, channels), 0)
-    sent_stat[...] = jnp.where(line == 0, tile_sum, tile_square)
+    sent_stat[...] = jnp.where(line == 0, mean * whole, jnp.where(line == 1, square, whole))
 
     @pl.loop(1, n)
     def _(s):
@@ -480,31 +547,25 @@
     def _(s):
         stat_copy(s).wait_recv()
 
-    def add_sum(t, carry):
-        total, units = carry
-        return total + all_stat[t, 0:1, :], units + valid_ref[t]
-
-    total, units = lax.fori_loop(
-        0, n, add_sum, (jnp.zeros((1, channels), F32), jnp.zeros((), jnp.int32))
-    )
-    total_count = units.astype(F32) * unit
-    mean = total / total_count
-
-    def add_square(t, square):
-        size = (valid_ref[t] * unit).astype(F32)
-        off = all_stat[t, 0:1, :] / size - mean
-        return square + all_stat[t, 1:2, :] + size * (off * off)
-
-    square = lax.fori_loop(0, n, add_square, jnp.zeros((1, channels), F32))
-    scale = gain_ref[...] * lax.rsqrt(square / total_count + 1e-05)
-    norm_ref[...] = jnp.where(
-        line == 0, mean, jnp.where(line == 1, scale, valid_ref[me].astype(F32))
-    )
+    mean, square, whole = combine(all_stat)
+    group_mean = group_total(mean) / group_size
+    off = mean - group_mean
+    group_square = group_total(square + whole * (off * off))
+    mean = group_mean
+    scale = gain_ref[...] * lax.rsqrt(group_square / (whole * group_size) + 1e-05)
+    sides = [(r, h) for r in range(2) for h in range(channels // 128)]
+    half_scale = 0.5 * scale
+    half_shift = 0.5 * (bias_ref[...] - mean * scale)
 
     @pl.loop(0, n)
     def _(f):
+        pixels = pl.ds(pl.multiple_of(f * 2 * row_tokens, 8), 2 * row_tokens)
+        live = f < valid_ref[me]
         for r, h in sides:
-            store(f, r, h).wait()
+            lanes = slice(h * 128, (h + 1) * 128)
+            normed = out_buf[r, h, pixels, :] * half_scale[:, lanes] + half_shift[:, lanes]
+            silu = normed + normed * jnp.tanh(normed)
+            decoded_ref[f, r, :, lanes] = jnp.where(live, silu, 0.0).astype(BF16)
 
     @pl.loop(0, chunks)
     def _(c):
@@ -521,12 +582,15 @@
         tok_copy(lax.rem(me + s, n)).wait_send()
         stat_copy(s).wait_send()
 
-    own_pass.wait_send()
-
-    @pl.loop(1, n // 2)
-    def _(k):
-        state_copy(k).wait_send()
-        state_pass(k).wait_send()
+    @pl.loop(1, levels)
+    def _(k):
+        column_copy(k).wait_send()
+
+    @pl.loop(0, levels)
+    def _(k):
+        row_pass(k).wait_send()
+        core_pass(k, 0).wait_send()
+        core_pass(k, 1).wait_send()
 
 
 def local(
@@ -546,18 +610,15 @@
     row_tokens = count // n
     chunks = count // CHUNK
     state_shape = (width // 128 * (width // HEADS) + 16, 128)
-    anywhere = pl.BlockSpec(memory_space=pl.ANY)
+    anywhere = pl.BlockSpec(memory_space=pltpu.HBM)
     vmem = pl.BlockSpec(memory_space=pltpu.VMEM)
     smem = pl.BlockSpec(memory_space=pltpu.SMEM)
     dma = pltpu.SemaphoreType.DMA
-    conv, norm = pl.pallas_call(
+    return pl.pallas_call(
         functools.partial(mega, n),
-        out_shape=(
-            jax.ShapeDtypeStruct((n, 2, 2 * row_tokens, channels), F32),
-            jax.ShapeDtypeStruct((8, channels), F32),
-        ),
-        in_specs=[anywhere] * 4 + [vmem, smem, vmem, smem],
-        out_specs=(anywhere, vmem),
+        out_shape=pltpu.VMEM((n, 2, 2 * row_tokens, channels), BF16),
+        in_specs=[anywhere] * 4 + [vmem, vmem, smem, vmem, smem],
+        out_specs=vmem,
         scratch_shapes=[
             pltpu.VMEM((count, width), BF16),
             pltpu.VMEM((width, 3 * width), BF16),
@@ -572,29 +633,30 @@
             pltpu.VMEM((n,) + state_shape, F32),
             pltpu.VMEM(state_shape, F32),
             pltpu.VMEM(state_shape, F32),
-            pltpu.VMEM((CHUNK, width), F32),
+            pltpu.VMEM((count, width), F32),
             pltpu.VMEM((2, count, 4 * channels), BF16),
             pltpu.VMEM((2, count, 2 * channels), BF16),
             pltpu.VMEM((2, count, 2 * channels), F32),
-            pltpu.VMEM((2, 8, channels), F32),
+            pltpu.VMEM((2 * chunks, 8, channels), F32),
             pltpu.VMEM((8, channels), F32),
             pltpu.VMEM((n, 8, channels), F32),
             pltpu.VMEM((2, channels // 128, 2 * count, 128), F32),
             dma((4,)),
             dma((n,)),
             dma((n,)),
-            dma((n // 2,)),
-            dma((n // 2,)),
-            dma((n // 2,)),
-            dma((n // 2,)),
+            dma((2, n // 4)),
+            dma((2, n // 4)),
+            dma((n // 4,)),
+            dma((n // 4,)),
+            dma((n // 4,)),
+            dma((n // 4,)),
             dma((2, chunks)),
             dma((2, chunks)),
             dma((n,)),
             dma((n,)),
-            dma((n, 2, channels // 128)),
         ],
         compiler_params=pltpu.CompilerParams(
-            collective_id=0, has_side_effects=True, vmem_limit_bytes=60 * 1024 * 1024
+            collective_id=0, has_side_effects=True, vmem_limit_bytes=VMEM - 2 * count * 4 * channels
         ),
     )(
         tokens,
@@ -602,13 +664,11 @@
         out_weight,
         conv_weight.reshape(3, 3 * channels, channels),
         norm_gain[None],
+        norm_bias[None],
         group_map,
         token_order[None],
         valid_frames,
     )
-    frame = lax.broadcasted_iota(jnp.int32, conv.shape, 0).astype(F32)
-    normed = (conv - norm[0]) * norm[1] + norm_bias
-    return jnp.where(frame < norm[2], jax.nn.silu(normed), 0.0).astype(BF16)
 
 
 def solution(mesh):

time: 70.8 us -> 61.8 us (0.87)
  other arithmetic: 4.9 us -> 0 us
  Pallas kernels: 64.8 us -> 60.3 us
    convert_element_type x2 -> x0, other arithmetic: 4.9 us -> none  [the longest x1 4.9 us: local(): return jnp.where(frame < norm[2], jax.nn.silu(normed), 0.0).astype(BF16)]
    pallas_call x1, Pallas kernels: 64.8 us -> 60.3 us  [local(): pl.pallas_call(functools.partial(mega, n), out_shape=pltpu.VMEM((n, 2, 2...]
    unnamed x2 -> x1, local copies, waits for them, and re-layouts: 0.01 us -> 1.32 us
    slice x1 -> x0, local copies, waits for them, and re-layouts: 0.81 us -> none  [local(): return jnp.where(frame < norm[2], jax.nn.silu(normed), 0.0).astype(BF16)]
where the time goes in v1:
time: 61.8 us; the launch traced here: 61.6 us
  Pallas kernels  60.3 us (98%)
  local copies, waits for them, and re-layouts  1.32 us (2%)
    pallas_call x1, Pallas kernels, local(): pl.pallas_call(functools.partial(mega, n), out_shape=pltpu.VMEM((n, 2, 2...  60.3 us
    unnamed x1, local copies, waits for them, and re-layouts  1.32 us

profile of v1, /device:TPU:0, one launch (start us, length us, event | category | flops | bytes accessed | tf_op | source)
XLA Modules:
  0.0 61.6 jit_solution(11933144087210708288)
XLA Ops:
  0.0 60.3 %shard_map.91 = bf16[16,2,128,256]{3,2,1,0:T(8,128)(2,1)S(1)} custom-call(bf16[1024,512]{1,0:T(8,128)(2,1)} %tokens_hbm.1, bf16[512,1536]{1,0:T(8,128)(2,1)} %qkv_hbm.1, bf16[512,1024]{1,0:T(8,128)(2,1)} %out_hbm.1, bf16[3,768,256]{2,1,0:T(8,128)(2,1)} %bitcast.4, f32[1,256]{1,0:T(1,128)} %bitcast.6, f32[1,256]{1,0:T(1,128)} %bitcast.7, s32[16]{0:T(128)} %group_ref.1, ...), custom_call_target="tpu_custom_call" | custom-call | tf_op jit(solution)/shard_map/pallas_call | solution.py:617
  60.3 1.3 %copy.11 = bf16[16,2,128,256]{3,2,1,0:T(8,128)(2,1)} copy(bf16[16,2,128,256]{3,2,1,0:T(8,128)(2,1)S(1)} %shard_map.91) | data formatting | bytes 4194304

commit v2 on v1

v2 whole, which is shorter than its diff:
```python
import functools

import jax
import jax.numpy as jnp
from jax import lax
from jax.experimental import pallas as pl
from jax.experimental.pallas import tpu as pltpu
from jax.sharding import PartitionSpec as P

HEADS = 16
NORM_GROUPS = 32
MESH = pl.DeviceIdType.MESH
F32 = jnp.float32
BF16 = jnp.bfloat16
CHUNK = 256
BLOCK = 256
VMEM = 66650112


def flat(cells):
    rows, width = cells.shape[-2:]
    every = cells.size // width
    if rows % 16 == 0:
        return cells.reshape(every, width)
    return cells.astype(F32).reshape(every, width).astype(BF16)


def mega(
    n,
    tokens_hbm,
    qkv_hbm,
    out_hbm,
    conv_hbm,
    gain_ref,
    bias_ref,
    group_ref,
    order_ref,
    valid_ref,
    decoded_ref,
    tokens_ref,
    qkv_ref,
    outw_ref,
    convw_ref,
    sent_tokens,
    tile_tokens,
    state_acc,
    sum_acc,
    sent_state,
    all_state,
    all_total,
    running,
    prefix,
    rows_ref,
    made,
    near_rows,
    cells,
    stat_acc,
    sent_stat,
    all_stat,
    out_buf,
    load_sem,
    tok_send,
    tok_recv,
    core_send,
    core_recv,
    col_send,
    col_recv,
    row_send,
    row_recv,
    made_send,
    relay_send,
    near_recv,
    stat_send,
    stat_recv,
):
    me = lax.axis_index("tm")
    count, width = tokens_ref.shape
    row_tokens = count // n
    pair_tokens = 2 * row_tokens
    chunks = count // CHUNK
    share = n // (2 * chunks)
    head_dim = width // HEADS
    channels = gain_ref.shape[1]
    blocks = width // BLOCK
    heads_per = BLOCK // head_dim
    group_size = channels // NORM_GROUPS

    levels = n // 4
    level = lax.div(me, 4)
    y = lax.rem(lax.div(me, 2), 2)
    core = lax.rem(me, 2)
    side = lax.div(me, n // 2)
    place = lax.div(me, n // chunks)
    inward = place + side * (chunks - 1 - 2 * place)
    inner = inward == 1
    mine = 2 * level + core
    core_peer = me + 1 - 2 * core
    row_peer = me + 2 - 4 * y

    def facing(k):
        return k + side * (chunks - 1 - 2 * k)

    def frame_of(source, column):
        return 4 * lax.div(source, 2) + 2 * column + lax.rem(source, 2)

    loads = [
        pltpu.make_async_copy(a, b, load_sem.at[i])
        for i, (a, b) in enumerate(
            [
                (tokens_hbm, tokens_ref),
                (qkv_hbm, qkv_ref),
                (out_hbm, outw_ref),
                (conv_hbm, convw_ref),
            ]
        )
    ]
    for load in loads:
        load.start()

    barrier = pltpu.get_barrier_semaphore()

    @pl.loop(1, n)
    def _(s):
        pl.semaphore_signal(
            barrier, inc=1, device_id={"tm": lax.rem(me + s, n)}, device_id_type=MESH
        )

    def remote(src, dst, send_sem, recv_sem, device):
        return pltpu.make_async_remote_copy(
            src_ref=src,
            dst_ref=dst,
            send_sem=send_sem,
            recv_sem=recv_sem,
            device_id={"tm": device},
            device_id_type=MESH,
        )

    def tok_copy(slot):
        return remote(
            sent_tokens.at[slot],
            tile_tokens.at[mine],
            tok_send.at[slot],
            tok_recv.at[mine],
            4 * lax.div(slot, 2) + 2 * y + lax.rem(slot, 2),
        )

    def tok_arrival(source):
        return remote(
            sent_tokens.at[source],
            tile_tokens.at[source],
            tok_send.at[source],
            tok_recv.at[source],
            4 * lax.div(source, 2) + 2 * y + lax.rem(source, 2),
        )

    def column_copy(k):
        return remote(
            sent_state,
            all_state.at[me],
            col_send.at[k],
            col_recv.at[k],
            lax.rem(me + 4 * k, n),
        )

    def pass_on(source, peer, send_sem, recv_sem):
        return remote(all_state.at[source], all_state.at[source], send_sem, recv_sem, peer)

    def row_pass(k):
        source = lax.rem(me + n - 4 * k, n)
        return pass_on(source, row_peer, row_send.at[k], row_recv.at[k])

    def core_pass(k, d):
        source = lax.rem(me + d * (row_peer - me) + n - 4 * k, n)
        return pass_on(source, core_peer, core_send.at[d, k], core_recv.at[d, k])

    def stat_copy(s):
        return remote(
            sent_stat,
            all_stat.at[me],
            stat_send.at[s],
            stat_recv.at[s],
            lax.rem(me + s, n),
        )

    across = lax.rem(y + core, 2)
    outer_owner = 4 * level + 3 * core
    inner_owner = 4 * level + 1 + core
    beyond = 4 * level - 1 + 5 * core
    exists = jnp.logical_and(beyond >= 0, beyond < n)
    beyond_device = jnp.clip(beyond, 0, n - 1)
    far_slot = 2 * core
    peer_slot = 2 - 2 * core

    def made_copy(kind, c):
        if kind == 0:
            part, device, slot = 1 - core, inner_owner, 1
        elif kind == 1:
            part, device, slot = core, beyond_device, peer_slot
        elif kind == 2:
            part = core
            device = across * outer_owner + (1 - across) * inner_owner
            slot = across + (1 - across) * far_slot
        else:
            part, device, slot = 1 - core, 4 * level + 2 - core, far_slot
        return remote(
            made.at[part, c],
            near_rows.at[slot, c, y],
            made_send.at[kind, c],
            near_recv.at[slot, c, y],
            device,
        )

    def relay_copy(c):
        return remote(
            near_rows.at[1, c, 1 - y],
            near_rows.at[far_slot, c, 1 - y],
            relay_send.at[c],
            near_recv.at[far_slot, c, 1 - y],
            core_peer,
        )

    def near_arrival(slot, c, column):
        return remote(
            near_rows.at[slot, c, column],
            near_rows.at[slot, c, column],
            made_send.at[0, c],
            near_recv.at[slot, c, column],
            core_peer,
        )

    loads[0].wait()

    def permute(to):
        where = lax.broadcasted_iota(jnp.int32, (CHUNK, count), 0) + to * CHUNK
        pick = jnp.where(order_ref[...] == where, 1.0, 0.0).astype(BF16)
        moved = jnp.dot(pick, tokens_ref[...], preferred_element_type=F32)
        sent_tokens[pl.ds(to * share, share)] = moved.reshape(share, pair_tokens, width).astype(
            BF16
        )

    def send_tiles(to):
        @pl.loop(0, share)
        def _(k):
            slot = to * share + k

            @pl.when(slot != mine)
            def _():
                tok_copy(slot).start()

    targets = [facing(x) for x in (inward + 1, inward * 0, 2 - inward, inward * 0 + 3)]

    loads[1].wait()
    state_acc[...] = jnp.zeros_like(state_acc)
    sum_acc[...] = jnp.zeros_like(sum_acc)

    @pl.loop(0, chunks)
    def _(c):
        rows = pl.ds(pl.multiple_of(c * CHUNK, CHUNK), CHUNK)
        mixed = jnp.dot(
            tokens_ref[rows, :], qkv_ref[:, width : 3 * width], preferred_element_type=F32
        ).astype(BF16)
        keys = jnp.maximum(mixed[:, :width], jnp.zeros((), BF16))
        sum_acc[...] += keys.astype(F32).reshape(CHUNK // 8, 8, width).sum(axis=0)
        for b in range(blocks):
            lanes = slice(b * BLOCK, (b + 1) * BLOCK)
            state_acc[b] += lax.dot_general(
                keys[:, lanes],
                mixed[:, width + b * BLOCK : width + (b + 1) * BLOCK],
                (((0,), (0,)), ((), ())),
                preferred_element_type=F32,
            )

    head_row = lax.broadcasted_iota(jnp.int32, (BLOCK, BLOCK), 0) // head_dim
    head_col = lax.broadcasted_iota(jnp.int32, (BLOCK, BLOCK), 1) // head_dim
    same_head = head_row == head_col
    pieces = width // 128
    sum_at = pieces * head_dim
    for b in range(blocks):
        own = jnp.where(same_head, state_acc[b], 0.0)
        own = own.reshape(heads_per, head_dim, BLOCK).sum(axis=0).astype(BF16)
        for i in range(BLOCK // 128):
            at = (b * (BLOCK // 128) + i) * head_dim
            sent_state[at : at + head_dim, :] = own[:, i * 128 : (i + 1) * 128]
    key_sum = jnp.sum(sum_acc[...], axis=0, keepdims=True)
    high = key_sum.astype(BF16).astype(F32)
    line = lax.broadcasted_iota(jnp.int32, (16, 128), 0)
    packed = jnp.zeros((16, 128), F32)
    for i in range(pieces):
        lanes = slice(i * 128, (i + 1) * 128)
        packed = jnp.where(line == i, high[:, lanes], packed)
        packed = jnp.where(line == pieces + i, (key_sum - high)[:, lanes], packed)
    sent_state[sum_at : sum_at + 16, :] = packed.astype(BF16)

    all_state[me] = sent_state[...]

    pl.semaphore_wait(barrier, n - 1)

    @pl.loop(1, levels)
    def _(k):
        column_copy(k).start()

    row_pass(0).start()
    core_pass(0, 0).start()

    permute(targets[0])
    send_tiles(targets[0])
    permute(targets[1])
    send_tiles(targets[1])

    @pl.loop(0, chunks // 2)
    def _(k):
        permute(facing((1 - k) * (2 - inward) + k * 3))

    tile_tokens[mine] = sent_tokens[mine]

    send_tiles(targets[2])
    send_tiles(targets[3])

    @pl.loop(1, levels)
    def _(k):
        column_copy(k).wait_recv()
        row_pass(k).start()
        core_pass(k, 0).start()

    @pl.loop(0, levels)
    def _(k):
        row_pass(k).wait_recv()
        core_pass(k, 1).start()

    def attend_order(k):
        if k < 2:
            return facing(inward + k * (1 - 2 * inward))
        return facing((3 - k) * (3 - inward) + (k - 2) * (2 + inward))

    def queries(c):
        @pl.loop(0, share)
        def _(k):
            source = c * share + k

            @pl.when(source != mine)
            def _():
                tok_arrival(source).wait_recv()

        mixed = jnp.dot(
            flat(tile_tokens[pl.ds(c * share, share)]),
            qkv_ref[:, 0:width],
            preferred_element_type=F32,
        ).astype(BF16)
        rows = pl.ds(pl.multiple_of(c * CHUNK, CHUNK), CHUNK)
        rows_ref[rows, :] = jnp.maximum(mixed, jnp.zeros((), BF16)).astype(F32)

    for k in range(2):
        queries(attend_order(k))

    @pl.loop(0, levels)
    def _(k):
        core_pass(k, 0).wait_recv()
        core_pass(k, 1).wait_recv()

    running[...] = jnp.zeros_like(running)
    prefix[...] = jnp.zeros_like(prefix)

    @pl.loop(0, n)
    def _(f):
        new_group = group_ref[f] != group_ref[jnp.maximum(f - 1, 0)]
        before = jnp.where(new_group, running[...], prefix[...])
        prefix[...] = before
        own = all_state[f].astype(F32)
        running[...] += own
        all_total[f] = before + own

    head_ones = same_head.astype(F32).astype(BF16)
    reach = 3 * channels

    def attend_chunk(c):
        rows = pl.ds(pl.multiple_of(c * CHUNK, CHUNK), CHUNK)

        def attend(k, carry):
            total = all_total[frame_of(c * share + k, y)]
            key_total = jnp.concatenate(
                [
                    total[sum_at + i : sum_at + i + 1, :]
                    + total[sum_at + pieces + i : sum_at + pieces + i + 1, :]
                    for i in range(pieces)
                ],
                axis=1,
            )
            here = pl.ds(pl.multiple_of(c * CHUNK + k * pair_tokens, 16), pair_tokens)
            query = rows_ref[here, :]
            scaled = (query * key_total).astype(BF16)
            query = query.astype(BF16)
            for b in range(blocks):
                lanes = slice(b * BLOCK, (b + 1) * BLOCK)
                first = b * (BLOCK // 128)
                state = jnp.concatenate(
                    [
                        total[i * head_dim : (i + 1) * head_dim, :]
                        for i in range(first, first + BLOCK // 128)
                    ],
                    axis=1,
                )
                high = state.astype(BF16).astype(F32)
                numer = jnp.zeros((pair_tokens, BLOCK), F32)
                for part in (high, state - high):
                    spread = jnp.concatenate([part] * heads_per, axis=0)
                    spread = jnp.where(same_head, spread, 0.0).astype(BF16)
                    numer += jnp.dot(query[:, lanes], spread, preferred_element_type=F32)
                denom = jnp.dot(scaled[:, lanes], head_ones, preferred_element_type=F32) + 1.0
                rows_ref[here, lanes] = numer / denom
            return carry

        lax.fori_loop(0, share, attend, 0, unroll=share <= 4)
        attended = rows_ref[rows, :].reshape(share, 2, row_tokens, width)
        for i in range(2):
            made[i, c] = attended[:, i].astype(BF16)
        made_copy(0, c).start()
        made_copy(2, c).start()

        @pl.when(across == 0)
        def _():
            made_copy(3, c).start()

        @pl.when(exists)
        def _():
            made_copy(1, c).start()

        @pl.when(across == 0)
        def _():
            near_rows[1, c, y] = made[core, c]
            near_rows[peer_slot, c, y] = made[1 - core, c]

        @pl.when(across == 1)
        def _():
            near_rows[far_slot, c, y] = made[1 - core, c]

    for k in range(2):
        attend_chunk(attend_order(k))

    loads[2].wait()
    loads[3].wait()

    def widen(even, odd):
        column = lax.rem(lax.broadcasted_iota(jnp.int32, even.shape, 0), row_tokens)
        odd_left = jnp.where(column == 0, 0.0, pltpu.roll(odd, 1, 0))
        even_right = jnp.where(column == row_tokens - 1, 0.0, pltpu.roll(even, CHUNK - 1, 0))
        return [x.astype(BF16) for x in (odd_left, even, odd, even_right)]

    valid = valid_ref[me]
    valid_above = jnp.where(me > 0, valid_ref[jnp.maximum(me - 1, 0)], 0)
    valid_below = jnp.where(me < n - 1, valid_ref[jnp.minimum(me + 1, n - 1)], 0)
    valid_rows = valid * row_tokens

    outer = across == 0
    half = 2 * channels
    limits = (valid_above, valid, valid, valid_below)

    def frames_here():
        row = lax.broadcasted_iota(jnp.int32, (CHUNK, channels), 0)
        step = lax.div(row, row_tokens)
        return lax.rem(step, share), lax.div(step, share)

    def chunk_frames(c):
        k, column = frames_here()
        return frame_of(c * share + k, column)

    def place_line(p, line, frame, limit):
        live = frame < limit
        even = jnp.where(live, line[:, :channels], 0.0)
        odd = jnp.where(live, line[:, channels:], 0.0)
        for i, part in enumerate(widen(even, odd)):
            cells[p, :, i * channels : (i + 1) * channels] = part

    def out_pixels(c, b):
        return pl.ds(c * 2 * CHUNK + b, CHUNK, 2)

    def gather_stats(c, r, results, live):
        eights = [x.reshape(CHUNK // 8, 8, channels).sum(axis=0) for x in results]
        total = jnp.sum(eights[0] + eights[1], axis=0, keepdims=True)
        size = jnp.clip(valid_rows - c * CHUNK, 0, CHUNK) * 2
        centre = total / jnp.maximum(size, 1).astype(F32)
        square = jnp.zeros((8, channels), F32)
        for x in results:
            off = jnp.where(live, x - centre, 0.0)
            square += (off * off).reshape(CHUNK // 8, 8, channels).sum(axis=0)
        square = jnp.sum(square, axis=0, keepdims=True)
        line = lax.broadcasted_iota(jnp.int32, (8, channels), 0)
        stat_acc[2 * c + r] = jnp.where(
            line == 0, total, jnp.where(line == 1, square, size.astype(F32))
        )

    def decode(c, defer):
        near_arrival(1, c, 1 - y).wait_recv()
        relay_copy(c).start()

        @pl.when(jnp.logical_not(outer))
        def _():
            near_arrival(1, c, y).wait_recv()
            near_arrival(peer_slot, c, y).wait_recv()
            near_arrival(far_slot, c, 1 - y).wait_recv()

        if not defer:

            @pl.when(jnp.logical_and(outer, exists))
            def _():
                near_arrival(far_slot, c, y).wait_recv()
                near_arrival(far_slot, c, 1 - y).wait_recv()

        frame = chunk_frames(c)
        own = jnp.dot(flat(near_rows[1, c]), outw_ref[...], preferred_element_type=F32)
        place_line(1, own[:, :half], frame, valid)
        place_line(2, own[:, half:], frame, valid)
        near_arrival(peer_slot, c, 1 - y).wait_recv()
        absent = outer if defer else jnp.logical_and(outer, jnp.logical_not(exists))
        for p, slot, low in ((0, 0, half), (3, 2, 0)):
            missing = jnp.logical_and(absent, far_slot == slot)

            @pl.when(missing)
            def _():
                cells[p] = jnp.zeros(cells.shape[1:], BF16)

            @pl.when(jnp.logical_not(missing))
            def _():
                line = jnp.dot(
                    flat(near_rows[slot, c]),
                    outw_ref[:, low : low + half],
                    preferred_element_type=F32,
                )
                place_line(p, line, frame, limits[p])

        live = frame < valid
        for r in range(2):
            results = []
            for b in range(2):
                lanes = slice(b * channels, b * channels + reach)
                result = sum(
                    jnp.dot(cells[r + d, :, lanes], convw_ref[d], preferred_element_type=F32)
                    for d in range(3)
                )
                result = jnp.where(live, result, 0.0)
                results.append(result)
                for h in range(0, channels, 128):
                    out_buf[r, h // 128, out_pixels(c, b), :] = result[:, h : h + 128]
            gather_stats(c, r, results, live)

    def finish(c):
        near_arrival(far_slot, c, y).wait_recv()
        near_arrival(far_slot, c, 1 - y).wait_recv()
        frame = chunk_frames(c)
        line = jnp.dot(
            flat(near_rows[far_slot, c]),
            outw_ref[:, pl.ds(pl.multiple_of((1 - core) * half, half), half)],
            preferred_element_type=F32,
        )
        place_line(0, line, frame, jnp.where(core == 0, valid_above, valid_below))
        live = frame < valid
        results = []
        for b in range(2):
            lanes = slice(b * channels, b * channels + reach)
            result = jnp.dot(cells[0, :, lanes], convw_ref[far_slot], preferred_element_type=F32)
            before = jnp.concatenate(
                [out_buf[core, h, out_pixels(c, b), :] for h in range(channels // 128)], axis=1
            )
            result = before + jnp.where(live, result, 0.0)
            results.append(result)
            for h in range(0, channels, 128):
                out_buf[core, h // 128, out_pixels(c, b), :] = result[:, h : h + 128]
        gather_stats(c, core, results, live)

    for k in range(2, 4):
        queries(attend_order(k))
        attend_chunk(attend_order(k))

    def decode_order(k):
        return facing(k + lax.div(k, 2))

    @pl.loop(0, 3)
    def _(k):
        decode(decode_order(k), True)

    @pl.when(jnp.logical_and(outer, exists))
    def _():
        @pl.loop(0, 3)
        def _(k):
            finish(decode_order(k))

    decode(facing(2), False)

    group_row = lax.broadcasted_iota(jnp.int32, (channels, channels), 0) // group_size
    group_col = lax.broadcasted_iota(jnp.int32, (channels, channels), 1) // group_size
    group_ones = jnp.where(group_row == group_col, 1.0, 0.0).astype(BF16)

    def group_total(sums):
        parts = []
        for _ in range(3):
            part = sums.astype(BF16)
            parts.append(part)
            sums = sums - part.astype(F32)
        line = lax.broadcasted_iota(jnp.int32, (16, channels), 0)
        stacked = jnp.zeros((16, channels), F32)
        for i, part in enumerate(parts):
            stacked = jnp.where(line == i, part.astype(F32), stacked)
        found = jnp.dot(stacked.astype(BF16), group_ones, preferred_element_type=F32)
        return found[0:1] + found[1:2] + found[2:3]

    def combine(field):
        total, square, size = [field[:, i, :] for i in range(3)]
        whole = jnp.sum(size, axis=0, keepdims=True)
        mean = jnp.sum(total, axis=0, keepdims=True) / whole
        off = total / jnp.maximum(size, 1.0) - mean
        return mean, jnp.sum(square + size * (off * off), axis=0, keepdims=True), whole

    mean, square, whole = combine(stat_acc)
    line = lax.broadcasted_iota(jnp.int32, (8, channels), 0)
    sent_stat[...] = jnp.where(line == 0, mean * whole, jnp.where(line == 1, square, whole))

    @pl.loop(1, n)
    def _(s):
        stat_copy(s).start()

    all_stat[me] = sent_stat[...]

    @pl.loop(1, n)
    def _(s):
        stat_copy(s).wait_recv()

    mean, square, whole = combine(all_stat)
    group_mean = group_total(mean) / group_size
    off = mean - group_mean
    group_square = group_total(square + whole * (off * off))
    mean = group_mean
    scale = gain_ref[...] * lax.rsqrt(group_square / (whole * group_size) + 1e-05)
    sides = [(r, h) for r in range(2) for h in range(channels // 128)]
    half_scale = 0.5 * scale
    half_shift = 0.5 * (bias_ref[...] - mean * scale)

    @pl.loop(0, n)
    def _(s):
        pixels = pl.ds(pl.multiple_of(s * 2 * row_tokens, 8), 2 * row_tokens)
        step = lax.rem(s, 2 * share)
        f = frame_of(lax.div(s, 2 * share) * share + lax.rem(step, share), lax.div(step, share))
        live = f < valid
        for r, h in sides:
            lanes = slice(h * 128, (h + 1) * 128)
            normed = out_buf[r, h, pixels, :] * half_scale[:, lanes] + half_shift[:, lanes]
            silu = normed + normed * jnp.tanh(normed)
            decoded_ref[f, r, :, lanes] = jnp.where(live, silu, 0.0).astype(BF16)

    @pl.loop(0, n // 2)
    def _(slot):
        @pl.when(slot != mine)
        def _():
            tok_copy(slot).wait_send()

    @pl.loop(0, chunks)
    def _(c):
        made_copy(0, c).wait_send()
        made_copy(2, c).wait_send()
        relay_copy(c).wait_send()

        @pl.when(across == 0)
        def _():
            made_copy(3, c).wait_send()

        @pl.when(exists)
        def _():
            made_copy(1, c).wait_send()

    @pl.loop(1, n)
    def _(s):
        stat_copy(s).wait_send()

    @pl.loop(1, levels)
    def _(k):
        column_copy(k).wait_send()

    @pl.loop(0, levels)
    def _(k):
        row_pass(k).wait_send()
        core_pass(k, 0).wait_send()
        core_pass(k, 1).wait_send()


def local(
    tokens,
    qkv_weight,
    out_weight,
    conv_weight,
    norm_gain,
    norm_bias,
    group_map,
    token_order,
    valid_frames,
):
    n = lax.axis_size("tm")
    count, width = tokens.shape
    channels = conv_weight.shape[3]
    row_tokens = count // n
    chunks = count // CHUNK
    share = n // (2 * chunks)
    state_shape = (width // 128 * (width // HEADS) + 16, 128)
    anywhere = pl.BlockSpec(memory_space=pltpu.HBM)
    vmem = pl.BlockSpec(memory_space=pltpu.VMEM)
    smem = pl.BlockSpec(memory_space=pltpu.SMEM)
    dma = pltpu.SemaphoreType.DMA
    return pl.pallas_call(
        functools.partial(mega, n),
        out_shape=pltpu.VMEM((n, 2, 2 * row_tokens, channels), BF16),
        in_specs=[anywhere] * 4 + [vmem, vmem, smem, vmem, smem],
        out_specs=vmem,
        scratch_shapes=[
            pltpu.VMEM((count, width), BF16),
            pltpu.VMEM((width, 3 * width), BF16),
            pltpu.VMEM((width, 4 * channels), BF16),
            pltpu.VMEM((3, 3 * channels, channels), BF16),
            pltpu.VMEM((n // 2, 2 * row_tokens, width), BF16),
            pltpu.VMEM((n // 2, 2 * row_tokens, width), BF16),
            pltpu.VMEM((width // BLOCK, BLOCK, BLOCK), F32),
            pltpu.VMEM((8, width), F32),
            pltpu.VMEM(state_shape, BF16),
            pltpu.VMEM((n,) + state_shape, BF16),
            pltpu.VMEM((n,) + state_shape, F32),
            pltpu.VMEM(state_shape, F32),
            pltpu.VMEM(state_shape, F32),
            pltpu.VMEM((count, width), F32),
            pltpu.VMEM((2, chunks, share, row_tokens, width), BF16),
            pltpu.VMEM((3, chunks, 2, share, row_tokens, width), BF16),
            pltpu.VMEM((4, CHUNK, 4 * channels), BF16),
            pltpu.VMEM((2 * chunks, 8, channels), F32),
            pltpu.VMEM((8, channels), F32),
            pltpu.VMEM((n, 8, channels), F32),
            pltpu.VMEM((2, channels // 128, 2 * count, 128), F32),
            dma((4,)),
            dma((n // 2,)),
            dma((n // 2,)),
            dma((2, n // 4)),
            dma((2, n // 4)),
            dma((n // 4,)),
            dma((n // 4,)),
            dma((n // 4,)),
            dma((n // 4,)),
            dma((4, chunks)),
            dma((chunks,)),
            dma((3, chunks, 2)),
            dma((n,)),
            dma((n,)),
        ],
        compiler_params=pltpu.CompilerParams(
            collective_id=0, has_side_effects=True, vmem_limit_bytes=VMEM - 2 * count * 4 * channels
        ),
    )(
        tokens,
        qkv_weight,
        out_weight,
        conv_weight.reshape(3, 3 * channels, channels),
        norm_gain[None],
        norm_bias[None],
        group_map,
        token_order[None],
        valid_frames,
    )


def solution(mesh):
    in_specs = (P(("clip", "tm"), None), P(), P(), P(), P(), P(), P("clip"), P("clip"), P("clip"))
    out_specs = P("clip", "tm", None, None)
    return jax.shard_map(local, mesh=mesh, in_specs=in_specs, out_specs=out_specs, check_vma=False)
```

time: 61.8 us -> 59.6 us (0.964)
  Pallas kernels: 60.3 us -> 58.1 us
    pallas_call x1, Pallas kernels: 60.3 us -> 58.1 us  [local(): pl.pallas_call(functools.partial(mega, n), out_shape=pltpu.VMEM((n, 2, 2...]
where the time goes in v2:
time: 59.6 us; the launch traced here: 59.4 us
  Pallas kernels  58.1 us (97%)
  local copies, waits for them, and re-layouts  1.32 us (2%)
    pallas_call x1, Pallas kernels, local(): pl.pallas_call(functools.partial(mega, n), out_shape=pltpu.VMEM((n, 2, 2...  58.1 us
    unnamed x1, local copies, waits for them, and re-layouts  1.32 us

profile of v2, /device:TPU:0, one launch (start us, length us, event | category | flops | bytes accessed | tf_op | source)
XLA Modules:
  0.0 59.4 jit_solution(8663182402225981319)
XLA Ops:
  0.0 58.1 %shard_map.91 = bf16[16,2,128,256]{3,2,1,0:T(8,128)(2,1)S(1)} custom-call(bf16[1024,512]{1,0:T(8,128)(2,1)} %tokens_hbm.1, bf16[512,1536]{1,0:T(8,128)(2,1)} %qkv_hbm.1, bf16[512,1024]{1,0:T(8,128)(2,1)} %out_hbm.1, bf16[3,768,256]{2,1,0:T(8,128)(2,1)} %bitcast.4, f32[1,256]{1,0:T(1,128)} %bitcast.6, f32[1,256]{1,0:T(1,128)} %bitcast.7, s32[16]{0:T(128)} %group_ref.1, ...), custom_call_target="tpu_custom_call" | custom-call | tf_op jit(solution)/shard_map/pallas_call | solution.py:705
  58.1 1.3 %copy.11 = bf16[16,2,128,256]{3,2,1,0:T(8,128)(2,1)} copy(bf16[16,2,128,256]{3,2,1,0:T(8,128)(2,1)S(1)} %shard_map.91) | data formatting | bytes 4194304

commit v3 on v2

--- a/solution.py
+++ b/solution.py
@@ -328,9 +328,11 @@
         core_pass(k, 1).start()
 
     def attend_order(k):
-        if k < 2:
-            return facing(inward + k * (1 - 2 * inward))
-        return facing((3 - k) * (3 - inward) + (k - 2) * (2 + inward))
+        late = lax.div(k, 2)
+        return facing(
+            (1 - late) * (inward + k * (1 - 2 * inward))
+            + late * ((3 - k) * (3 - inward) + (k - 2) * (2 + inward))
+        )
 
     def queries(c):
         @pl.loop(0, share)
@@ -420,10 +422,6 @@
         def _():
             made_copy(3, c).start()
 
-        @pl.when(exists)
-        def _():
-            made_copy(1, c).start()
-
         @pl.when(across == 0)
         def _():
             near_rows[1, c, y] = made[core, c]
@@ -488,10 +486,11 @@
             line == 0, total, jnp.where(line == 1, square, size.astype(F32))
         )
 
-    def decode(c, defer):
+    def relay(c):
         near_arrival(1, c, 1 - y).wait_recv()
         relay_copy(c).start()
 
+    def decode(c, defer):
         @pl.when(jnp.logical_not(outer))
         def _():
             near_arrival(1, c, y).wait_recv()
@@ -566,24 +565,55 @@
                 out_buf[core, h // 128, out_pixels(c, b), :] = result[:, h : h + 128]
         gather_stats(c, core, results, live)
 
-    for k in range(2, 4):
-        queries(attend_order(k))
-        attend_chunk(attend_order(k))
-
-    def decode_order(k):
-        return facing(k + lax.div(k, 2))
-
-    @pl.loop(0, 3)
-    def _(k):
-        decode(decode_order(k), True)
+    def reach_beyond(*steps):
+        @pl.when(exists)
+        def _():
+            for k in steps:
+                made_copy(1, attend_order(k)).start()
+
+    def first_decode():
+        decode(attend_order(0), True)
+
+    @pl.when(jnp.logical_and(inner, core == 1))
+    def _():
+        relay(attend_order(0))
+        first_decode()
+
+    @pl.when(jnp.logical_not(inner))
+    def _():
+        relay(attend_order(0))
+
+    queries(attend_order(2))
+    attend_chunk(attend_order(2))
+    reach_beyond(0, 1)
+
+    @pl.when(jnp.logical_not(inner))
+    def _():
+        first_decode()
+
+    queries(attend_order(3))
+    attend_chunk(attend_order(3))
+    reach_beyond(2, 3)
+
+    @pl.when(jnp.logical_and(inner, core == 0))
+    def _():
+        relay(attend_order(0))
+        first_decode()
+
+    relay(attend_order(1))
+
+    decode(attend_order(1), True)
+    relay(attend_order(2))
+    decode(attend_order(2), True)
 
     @pl.when(jnp.logical_and(outer, exists))
     def _():
         @pl.loop(0, 3)
         def _(k):
-            finish(decode_order(k))
-
-    decode(facing(2), False)
+            finish(attend_order(k))
+
+    relay(attend_order(3))
+    decode(attend_order(3), False)
 
     group_row = lax.broadcasted_iota(jnp.int32, (channels, channels), 0) // group_size
     group_col = lax.broadcasted_iota(jnp.int32, (channels, channels), 1) // group_size

time: 59.6 us -> 57 us (0.956)
  Pallas kernels: 58.1 us -> 55.5 us
    pallas_call x1, Pallas kernels: 58.1 us -> 55.5 us  [local(): pl.pallas_call(functools.partial(mega, n), out_shape=pltpu.VMEM((n, 2, 2...]
where the time goes in v3:
time: 57 us; the launch traced here: 56.8 us
  Pallas kernels  55.5 us (97%)
  local copies, waits for them, and re-layouts  1.32 us (2%)
    pallas_call x1, Pallas kernels, local(): pl.pallas_call(functools.partial(mega, n), out_shape=pltpu.VMEM((n, 2, 2...  55.5 us
    unnamed x1, local copies, waits for them, and re-layouts  1.32 us

profile of v3, /device:TPU:0, one launch (start us, length us, event | category | flops | bytes accessed | tf_op | source)
XLA Modules:
  0.0 56.8 jit_solution(10139536975653042525)
XLA Ops:
  0.0 55.5 %shard_map.91 = bf16[16,2,128,256]{3,2,1,0:T(8,128)(2,1)S(1)} custom-call(bf16[1024,512]{1,0:T(8,128)(2,1)} %tokens_hbm.1, bf16[512,1536]{1,0:T(8,128)(2,1)} %qkv_hbm.1, bf16[512,1024]{1,0:T(8,128)(2,1)} %out_hbm.1, bf16[3,768,256]{2,1,0:T(8,128)(2,1)} %bitcast.4, f32[1,256]{1,0:T(1,128)} %bitcast.6, f32[1,256]{1,0:T(1,128)} %bitcast.7, s32[16]{0:T(128)} %group_ref.1, ...), custom_call_target="tpu_custom_call" | custom-call | tf_op jit(solution)/shard_map/pallas_call | solution.py:735
  55.5 1.3 %copy.11 = bf16[16,2,128,256]{3,2,1,0:T(8,128)(2,1)} copy(bf16[16,2,128,256]{3,2,1,0:T(8,128)(2,1)S(1)} %shard_map.91) | data formatting | bytes 4194304

commit v4 on v3

--- a/solution.py
+++ b/solution.py
@@ -351,8 +351,7 @@
         rows = pl.ds(pl.multiple_of(c * CHUNK, CHUNK), CHUNK)
         rows_ref[rows, :] = jnp.maximum(mixed, jnp.zeros((), BF16)).astype(F32)
 
-    for k in range(2):
-        queries(attend_order(k))
+    queries(attend_order(0))
 
     @pl.loop(0, levels)
     def _(k):
@@ -431,8 +430,9 @@
         def _():
             near_rows[far_slot, c, y] = made[1 - core, c]
 
-    for k in range(2):
-        attend_chunk(attend_order(k))
+    attend_chunk(attend_order(0))
+    queries(attend_order(1))
+    attend_chunk(attend_order(1))
 
     loads[2].wait()
     loads[3].wait()
@@ -576,6 +576,7 @@
 
     @pl.when(jnp.logical_and(inner, core == 1))
     def _():
+        reach_beyond(0, 1)
         relay(attend_order(0))
         first_decode()
 
@@ -585,7 +586,10 @@
 
     queries(attend_order(2))
     attend_chunk(attend_order(2))
-    reach_beyond(0, 1)
+
+    @pl.when(jnp.logical_not(jnp.logical_and(inner, core == 1)))
+    def _():
+        reach_beyond(0, 1)
 
     @pl.when(jnp.logical_not(inner))
     def _():
@@ -632,20 +636,24 @@
         found = jnp.dot(stacked.astype(BF16), group_ones, preferred_element_type=F32)
         return found[0:1] + found[1:2] + found[2:3]
 
-    def combine(field):
-        total, square, size = [field[:, i, :] for i in range(3)]
+    def combine(total, square, size):
         whole = jnp.sum(size, axis=0, keepdims=True)
         mean = jnp.sum(total, axis=0, keepdims=True) / whole
         off = total / jnp.maximum(size, 1.0) - mean
         return mean, jnp.sum(square + size * (off * off), axis=0, keepdims=True), whole
 
-    mean, square, whole = combine(stat_acc)
-    line = lax.broadcasted_iota(jnp.int32, (8, channels), 0)
-    sent_stat[...] = jnp.where(line == 0, mean * whole, jnp.where(line == 1, square, whole))
+    mean, square, whole = combine(*[stat_acc[:, i, :] for i in range(3)])
+    halves = channels // 128
+    line = lax.broadcasted_iota(jnp.int32, (8, 128), 0)
+    packed = jnp.zeros((8, 128), F32)
+    for i, field in enumerate((mean * whole, square, whole)):
+        for h in range(halves):
+            packed = jnp.where(line == i * halves + h, field[:, h * 128 : (h + 1) * 128], packed)
+    sent_stat[...] = packed
 
     @pl.loop(1, n)
     def _(s):
-        stat_copy(s).start()
+        stat_copy(s + (1 - side) * (n - 2 * s)).start()
 
     all_stat[me] = sent_stat[...]
 
@@ -653,7 +661,12 @@
     def _(s):
         stat_copy(s).wait_recv()
 
-    mean, square, whole = combine(all_stat)
+    mean, square, whole = combine(
+        *[
+            jnp.concatenate([all_stat[:, i * halves + h, :] for h in range(halves)], axis=1)
+            for i in range(3)
+        ]
+    )
     group_mean = group_total(mean) / group_size
     off = mean - group_mean
     group_square = group_total(square + whole * (off * off))
@@ -756,8 +769,8 @@
             pltpu.VMEM((3, chunks, 2, share, row_tokens, width), BF16),
             pltpu.VMEM((4, CHUNK, 4 * channels), BF16),
             pltpu.VMEM((2 * chunks, 8, channels), F32),
-            pltpu.VMEM((8, channels), F32),
-            pltpu.VMEM((n, 8, channels), F32),
+            pltpu.VMEM((8, 128), F32),
+            pltpu.VMEM((n, 8, 128), F32),
             pltpu.VMEM((2, channels // 128, 2 * count, 128), F32),
             dma((4,)),
             dma((n // 2,)),

time: 57 us -> 57 us (level)
  no operation moved by 1% of the time
where the time goes in v4:
time: 57 us; the launch traced here: 56.8 us
  Pallas kernels  55.5 us (97%)
  local copies, waits for them, and re-layouts  1.32 us (2%)
    pallas_call x1, Pallas kernels, local(): pl.pallas_call(functools.partial(mega, n), out_shape=pltpu.VMEM((n, 2, 2...  55.5 us
    unnamed x1, local copies, waits for them, and re-layouts  1.32 us

profile of v4, /device:TPU:0, one launch (start us, length us, event | category | flops | bytes accessed | tf_op | source)
XLA Modules:
  0.0 56.8 jit_solution(12470190822613702756)
XLA Ops:
  0.0 55.5 %shard_map.91 = bf16[16,2,128,256]{3,2,1,0:T(8,128)(2,1)S(1)} custom-call(bf16[1024,512]{1,0:T(8,128)(2,1)} %tokens_hbm.1, bf16[512,1536]{1,0:T(8,128)(2,1)} %qkv_hbm.1, bf16[512,1024]{1,0:T(8,128)(2,1)} %out_hbm.1, bf16[3,768,256]{2,1,0:T(8,128)(2,1)} %bitcast.4, f32[1,256]{1,0:T(1,128)} %bitcast.6, f32[1,256]{1,0:T(1,128)} %bitcast.7, s32[16]{0:T(128)} %group_ref.1, ...), custom_call_target="tpu_custom_call" | custom-call | tf_op jit(solution)/shard_map/pallas_call | solution.py:748
  55.5 1.3 %copy.11 = bf16[16,2,128,256]{3,2,1,0:T(8,128)(2,1)} copy(bf16[16,2,128,256]{3,2,1,0:T(8,128)(2,1)S(1)} %shard_map.91) | data formatting | bytes 4194304

commit v5 on v4

--- a/solution.py
+++ b/solution.py
@@ -612,11 +612,16 @@
 
     @pl.when(jnp.logical_and(outer, exists))
     def _():
-        @pl.loop(0, 3)
+        @pl.loop(0, 2)
         def _(k):
             finish(attend_order(k))
 
     relay(attend_order(3))
+
+    @pl.when(jnp.logical_and(outer, exists))
+    def _():
+        finish(attend_order(2))
+
     decode(attend_order(3), False)
 
     group_row = lax.broadcasted_iota(jnp.int32, (channels, channels), 0) // group_size

time: 57 us -> 56.2 us (0.986)
  Pallas kernels: 55.5 us -> 54.7 us
    pallas_call x1, Pallas kernels: 55.5 us -> 54.7 us  [local(): pl.pallas_call(functools.partial(mega, n), out_shape=pltpu.VMEM((n, 2, 2...]
where the time goes in v5:
time: 56.2 us; the launch traced here: 56 us
  Pallas kernels  54.7 us (97%)
  local copies, waits for them, and re-layouts  1.32 us (2%)
    pallas_call x1, Pallas kernels, local(): pl.pallas_call(functools.partial(mega, n), out_shape=pltpu.VMEM((n, 2, 2...  54.7 us
    unnamed x1, local copies, waits for them, and re-layouts  1.32 us

profile of v5, /device:TPU:0, one launch (start us, length us, event | category | flops | bytes accessed | tf_op | source)
XLA Modules:
  0.0 56.0 jit_solution(8194034933791098030)
XLA Ops:
  0.0 54.7 %shard_map.91 = bf16[16,2,128,256]{3,2,1,0:T(8,128)(2,1)S(1)} custom-call(bf16[1024,512]{1,0:T(8,128)(2,1)} %tokens_hbm.1, bf16[512,1536]{1,0:T(8,128)(2,1)} %qkv_hbm.1, bf16[512,1024]{1,0:T(8,128)(2,1)} %out_hbm.1, bf16[3,768,256]{2,1,0:T(8,128)(2,1)} %bitcast.4, f32[1,256]{1,0:T(1,128)} %bitcast.6, f32[1,256]{1,0:T(1,128)} %bitcast.7, s32[16]{0:T(128)} %group_ref.1, ...), custom_call_target="tpu_custom_call" | custom-call | tf_op jit(solution)/shard_map/pallas_call | solution.py:753
  54.7 1.3 %copy.11 = bf16[16,2,128,256]{3,2,1,0:T(8,128)(2,1)} copy(bf16[16,2,128,256]{3,2,1,0:T(8,128)(2,1)S(1)} %shard_map.91) | data formatting | bytes 4194304

commit v6 on v5

--- a/solution.py
+++ b/solution.py
@@ -662,6 +662,36 @@
 
     all_stat[me] = sent_stat[...]
 
+    @pl.loop(0, n // 2)
+    def _(slot):
+        @pl.when(slot != mine)
+        def _():
+            tok_copy(slot).wait_send()
+
+    @pl.loop(0, chunks)
+    def _(c):
+        made_copy(0, c).wait_send()
+        made_copy(2, c).wait_send()
+        relay_copy(c).wait_send()
+
+        @pl.when(across == 0)
+        def _():
+            made_copy(3, c).wait_send()
+
+        @pl.when(exists)
+        def _():
+            made_copy(1, c).wait_send()
+
+    @pl.loop(1, levels)
+    def _(k):
+        column_copy(k).wait_send()
+
+    @pl.loop(0, levels)
+    def _(k):
+        row_pass(k).wait_send()
+        core_pass(k, 0).wait_send()
+        core_pass(k, 1).wait_send()
+
     @pl.loop(1, n)
     def _(s):
         stat_copy(s).wait_recv()
@@ -693,39 +723,9 @@
             silu = normed + normed * jnp.tanh(normed)
             decoded_ref[f, r, :, lanes] = jnp.where(live, silu, 0.0).astype(BF16)
 
-    @pl.loop(0, n // 2)
-    def _(slot):
-        @pl.when(slot != mine)
-        def _():
-            tok_copy(slot).wait_send()
-
-    @pl.loop(0, chunks)
-    def _(c):
-        made_copy(0, c).wait_send()
-        made_copy(2, c).wait_send()
-        relay_copy(c).wait_send()
-
-        @pl.when(across == 0)
-        def _():
-            made_copy(3, c).wait_send()
-
-        @pl.when(exists)
-        def _():
-            made_copy(1, c).wait_send()
-
     @pl.loop(1, n)
     def _(s):
         stat_copy(s).wait_send()
-
-    @pl.loop(1, levels)
-    def _(k):
-        column_copy(k).wait_send()
-
-    @pl.loop(0, levels)
-    def _(k):
-        row_pass(k).wait_send()
-        core_pass(k, 0).wait_send()
-        core_pass(k, 1).wait_send()
 
 
 def local(

time: 56.2 us -> 56 us (level)
  no operation moved by 1% of the time
where the time goes in v6:
time: 56 us; the launch traced here: 55.8 us
  Pallas kernels  54.5 us (97%)
  local copies, waits for them, and re-layouts  1.32 us (2%)
    pallas_call x1, Pallas kernels, local(): pl.pallas_call(functools.partial(mega, n), out_shape=pltpu.VMEM((n, 2, 2...  54.5 us
    unnamed x1, local copies, waits for them, and re-layouts  1.32 us

profile of v6, /device:TPU:0, one launch (start us, length us, event | category | flops | bytes accessed | tf_op | source)
XLA Modules:
  0.0 55.8 jit_solution(11514086783882261816)
XLA Ops:
  0.0 54.5 %shard_map.91 = bf16[16,2,128,256]{3,2,1,0:T(8,128)(2,1)S(1)} custom-call(bf16[1024,512]{1,0:T(8,128)(2,1)} %tokens_hbm.1, bf16[512,1536]{1,0:T(8,128)(2,1)} %qkv_hbm.1, bf16[512,1024]{1,0:T(8,128)(2,1)} %out_hbm.1, bf16[3,768,256]{2,1,0:T(8,128)(2,1)} %bitcast.4, f32[1,256]{1,0:T(1,128)} %bitcast.6, f32[1,256]{1,0:T(1,128)} %bitcast.7, s32[16]{0:T(128)} %group_ref.1, ...), custom_call_target="tpu_custom_call" | custom-call | tf_op jit(solution)/shard_map/pallas_call | solution.py:753
  54.5 1.3 %copy.11 = bf16[16,2,128,256]{3,2,1,0:T(8,128)(2,1)} copy(bf16[16,2,128,256]{3,2,1,0:T(8,128)(2,1)S(1)} %shard_map.91) | data formatting | bytes 4194304

commit v7 on v6

--- a/solution.py
+++ b/solution.py
@@ -612,15 +612,15 @@
 
     @pl.when(jnp.logical_and(outer, exists))
     def _():
-        @pl.loop(0, 2)
+        finish(attend_order(0))
+
+    relay(attend_order(3))
+
+    @pl.when(jnp.logical_and(outer, exists))
+    def _():
+        @pl.loop(1, 3)
         def _(k):
             finish(attend_order(k))
-
-    relay(attend_order(3))
-
-    @pl.when(jnp.logical_and(outer, exists))
-    def _():
-        finish(attend_order(2))
 
     decode(attend_order(3), False)
 

time: 56 us -> 55.7 us (level)
  no operation moved by 1% of the time
where the time goes in v7:
time: 55.7 us; the launch traced here: 55.6 us
  Pallas kernels  54.2 us (97%)
  local copies, waits for them, and re-layouts  1.32 us (2%)
    pallas_call x1, Pallas kernels, local(): pl.pallas_call(functools.partial(mega, n), out_shape=pltpu.VMEM((n, 2, 2...  54.2 us
    unnamed x1, local copies, waits for them, and re-layouts  1.32 us

profile of v7, /device:TPU:0, one launch (start us, length us, event | category | flops | bytes accessed | tf_op | source)
XLA Modules:
  0.0 55.6 jit_solution(14221967284910800635)
XLA Ops:
  0.0 54.2 %shard_map.91 = bf16[16,2,128,256]{3,2,1,0:T(8,128)(2,1)S(1)} custom-call(bf16[1024,512]{1,0:T(8,128)(2,1)} %tokens_hbm.1, bf16[512,1536]{1,0:T(8,128)(2,1)} %qkv_hbm.1, bf16[512,1024]{1,0:T(8,128)(2,1)} %out_hbm.1, bf16[3,768,256]{2,1,0:T(8,128)(2,1)} %bitcast.4, f32[1,256]{1,0:T(1,128)} %bitcast.6, f32[1,256]{1,0:T(1,128)} %bitcast.7, s32[16]{0:T(128)} %group_ref.1, ...), custom_call_target="tpu_custom_call" | custom-call | tf_op jit(solution)/shard_map/pallas_call | solution.py:753
  54.3 1.3 %copy.11 = bf16[16,2,128,256]{3,2,1,0:T(8,128)(2,1)} copy(bf16[16,2,128,256]{3,2,1,0:T(8,128)(2,1)S(1)} %shard_map.91) | data formatting | bytes 4194304
